TPU v7x, 256 devices: a whole 4x4x8 slice. The times are simulated.
256 devices in a mesh: grp: 4 (over z_hi), gx: 4 (over x), gy: 16 (over z_lo, y, core).
Axes of the slice: x: 4, y: 4, z: 8 (z_hi: 4, z_lo: 2; z = z_hi * 2 + z_lo), core: 2. Of those that a mesh axis runs over, the one named last changes fastest.
Arguments:
- state: float32 [4, 5, 16, 64, 2048], P('grp', None, None, 'gx', 'gy'), as said below
- view_dir: int32 [64], P('gx'), may hold values from 0 to 1
Outputs:
- new_state: float32 [4, 5, 16, 64, 2048], P('grp', None, None, 'gx', 'gy')
- side_view: float32 [4, 64, 3, 16], P('grp', 'gx', None, 'gy')
- occupancy_fine: bfloat16 [4, 12, 16, 512], P('grp', None, 'gx', 'gy')
- occupancy_coarse: bfloat16 [4, 3, 4, 128], P('grp', None, 'gx', 'gy')
Inputs may be any that keep to these rules, and one draw needn't show every extreme that they name: `state`: in every cell the density is positive and the pressure 0.4 (field 4 - (field 1 squared + field 2 squared + field 3 squared) / (2 field 0)) is positive.
All inputs are finite; a program needn't handle non-finite values.
Results may differ from a plain program's by a relative error of at most 0.0035.
The roundings to bfloat16 on the way count: a program that leaves them out, or rounds other values in their place, can miss the bound.
Values may be sent and summed in bfloat16 or wider, within the bound.
A program may use at most 64 MiB of HBM per device.

v0:
```python
import jax
import jax.numpy as jnp
from jax import lax
from jax.sharding import PartitionSpec as P

gamma_gas = 1.4
courant = 0.8


def swapped(shard, axis, distance):
    return lax.ppermute(shard, axis, [(i, i ^ 1 << distance) for i in range(lax.axis_size(axis))])


def padded_2(shard, sides, width):
    for axis, dim in sides:
        count, length = (lax.axis_size(axis), shard.shape[dim])
        up = [(i, (i + 1) % count) for i in range(count)]
        down = [(j, i) for i, j in up]
        last = lax.slice_in_dim(shard, length - width, length, axis=dim)
        first = lax.slice_in_dim(shard, 0, width, axis=dim)
        before = lax.ppermute(last, axis, up)
        after = lax.ppermute(first, axis, down)
        shard = jnp.concatenate([before, shard, after], axis=dim)
    return shard


def minmod(backward, forward):
    return jnp.maximum(0.0, jnp.minimum(backward, forward)) + jnp.minimum(
        0.0, jnp.maximum(backward, forward)
    )


def primitive(fields):
    fluid_rho_field = fields[0]
    velocity = fields[1:4] / fluid_rho_field
    fluid_stress_field = (gamma_gas - 1.0) * (
        fields[4] - 0.5 * jnp.sum(fields[1:4] * velocity, axis=0)
    )
    return jnp.concatenate([fluid_rho_field[None], velocity, fluid_stress_field[None]], axis=0)


def conserved(states):
    fluid_rho_field = states[0]
    momentum = states[1:4] * fluid_rho_field
    energy = states[4] / (gamma_gas - 1.0) + 0.5 * jnp.sum(momentum * states[1:4], axis=0)
    return jnp.concatenate([fluid_rho_field[None], momentum, energy[None]], axis=0)


def physical_flux(states, fields, normal):
    normal_speed = states[normal]
    fluid_stress_field = states[4]
    extra = (
        jnp.zeros_like(fields)
        .at[normal]
        .set(fluid_stress_field)
        .at[4]
        .set(fluid_stress_field * normal_speed)
    )
    return fields * normal_speed + extra


def sound_reach(states, normal):
    return jnp.abs(states[normal]) + jnp.sqrt(gamma_gas * states[4] / states[0])


def slice_along(values, start, length, direction):
    return lax.slice_in_dim(values, start, start + length, axis=direction)


def divergence(padded, direction):
    length = padded.shape[direction] - 4
    states = primitive(padded)
    differences = slice_along(states, 1, length + 3, direction) - slice_along(
        states, 0, length + 3, direction
    )
    slopes = minmod(
        slice_along(differences, 0, length + 2, direction),
        slice_along(differences, 1, length + 2, direction),
    )
    lower_state = slice_along(states, 1, length + 1, direction) + 0.5 * slice_along(
        slopes, 0, length + 1, direction
    )
    upper_state = slice_along(states, 2, length + 1, direction) - 0.5 * slice_along(
        slopes, 1, length + 1, direction
    )
    lower_fields = conserved(lower_state)
    upper_fields = conserved(upper_state)
    wave_speed = jnp.maximum(
        sound_reach(lower_state, direction), sound_reach(upper_state, direction)
    )
    face_flux = 0.5 * (
        physical_flux(lower_state, lower_fields, direction)
        + physical_flux(upper_state, upper_fields, direction)
    ) - 0.5 * wave_speed * (upper_fields - lower_fields)
    return slice_along(face_flux, 1, length, direction) - slice_along(
        face_flux, 0, length, direction
    )


def advance_block(padded, time_step):
    inner = padded[:, 2:-2, 2:-2, 2:-2]
    change = divergence(padded[:, :, 2:-2, 2:-2], 1)
    change = change + divergence(padded[:, 2:-2, :, 2:-2], 2)
    change = change + divergence(padded[:, 2:-2, 2:-2, :], 3)
    return inner - time_step * change


def max_speed(fields):
    states = primitive(fields)
    return jnp.max(
        jnp.sum(jnp.abs(states[1:4]), axis=0) + 3.0 * jnp.sqrt(gamma_gas * states[4] / states[0])
    )


def pool_once(volume):
    num_planes, num_rows, num_cols = volume.shape
    return jnp.max(
        volume.reshape(num_planes // 2, 2, num_rows // 2, 2, num_cols // 2, 2), axis=(1, 3, 5)
    )


def project(volume, attenuation):
    return jnp.max(volume.astype(jnp.float32) * attenuation[None], axis=2)


def composite(image):
    rounds = lax.axis_size("gy").bit_length() - 1
    position = lax.axis_index("gy")
    result = image
    for bit_number in reversed(range(rounds)):
        half_width = result.shape[2] // 2
        lower_half = result[:, :, :half_width]
        upper_half = result[:, :, half_width:]
        upper_kept = position >> bit_number & 1 == 1
        outgoing = jnp.where(upper_kept, lower_half, upper_half)
        keep_half = jnp.where(upper_kept, upper_half, lower_half)
        result = jnp.maximum(keep_half, swapped(outgoing, "gy", bit_number))
    return result


def body(state, view_dir):
    fields = state[0]
    slab_count = lax.axis_size("grp") - 1
    visual = lax.axis_index("grp") == slab_count
    padded = padded_2(fields, (("grp", 1), ("gx", 2), ("gy", 3)), 2)
    top_speed = lax.pmax(max_speed(fields), ("grp", "gx", "gy"))
    advanced = advance_block(padded, courant / top_speed)
    new_state = jnp.where(visual, fields, advanced)[None]
    snapshot = advanced[0].astype(jnp.bfloat16)
    planes, width_x, width_y = snapshot.shape
    columns = lax.axis_size("gy")
    fraction = (lax.axis_index("gy") * width_y + jnp.arange(width_y, dtype=jnp.int32)).astype(
        jnp.float32
    ) / jnp.float32(width_y * columns - 1)
    toward = jnp.exp(-fraction)
    away_side = jnp.exp(-(1.0 - fraction))
    attenuation = jnp.where(view_dir[:, None] == 0, toward[None, :], away_side[None, :])
    blocks = lax.all_gather(snapshot, "grp", axis=0, tiled=True)
    column = blocks[: slab_count * planes]
    image = project(column, attenuation).T.reshape(width_x, slab_count, planes)
    view_tile = composite(image)
    fine = pool_once(pool_once(column))
    coarse = pool_once(pool_once(fine))
    side_view = jnp.where(visual, view_tile, jnp.zeros_like(view_tile))[None]
    occupancy_fine = jnp.where(visual, fine, jnp.zeros_like(fine))[None]
    occupancy_coarse = jnp.where(visual, coarse, jnp.zeros_like(coarse))[None]
    return (new_state, side_view, occupancy_fine, occupancy_coarse)


def solution(mesh):
    in_specs = (P("grp", None, None, "gx", "gy"), P("gx"))
    out_specs = (
        P("grp", None, None, "gx", "gy"),
        P("grp", "gx", None, "gy"),
        P("grp", None, "gx", "gy"),
        P("grp", None, "gx", "gy"),
    )
    return jax.shard_map(body, mesh=mesh, in_specs=in_specs, out_specs=out_specs, check_vma=False)
```

profile of v0, /device:TPU:1, one launch (start us, length us, event | category | flops | bytes accessed | tf_op | source)
XLA Modules:
  0.0 189.6 jit_solution(10455681546007368053)
XLA Ops:
  0.6 1.0 fusion.28
  1.7 3.9 %collective-permute-start = (f32[5,2,16,128]{3,2,1,0:T(8,128)S(1)}, f32[5,2,16,128]{3,2,1,0:T(8,128)S(1)}, u32[]{:S(2)}, u32[]{:S(2)}) collective-permute-start(f32[5,2,16,128]{3,2,1,0:T(8,128)S(1)} %get-tuple-element.229), channel_id=1, source_target_pairs={{0,64},{64,128},{128,192},{192,0},{1,65},{65,129},{129,193},{193,1... | collective-permute-start | bytes 245768 | tf_op jit(solution)/shard_map/ppermute | solution.py:21
  5.5 3.1 %collective-permute-start.1 = (f32[5,2,16,128]{3,2,1,0:T(8,128)S(1)}, f32[5,2,16,128]{3,2,1,0:T(8,128)S(1)}, u32[]{:S(2)}, u32[]{:S(2)}) collective-permute-start(f32[5,2,16,128]{3,2,1,0:T(8,128)S(1)} %get-tuple-element.230), channel_id=1, source_target_pairs={{64,0},{128,64},{192,128},{0,192},{65,1},{129,65},{193,129},{1,193... | collective-permute-start | bytes 245768 | tf_op jit(solution)/shard_map/ppermute | solution.py:22
  8.7 0.9 slice_bitcast_fusion.4
  9.6 0.7 broadcast_compare_fusion
  10.3 1.1 fusion.11
  11.4 0.7 fusion.21
  12.1 76.8 %pmax.7 = f32[]{:T(128)} all-reduce(f32[]{:T(128)} %fusion.21), channel_id=1, replica_groups=mesh['grp'=4,'gx'=4,'gy'=16] {'grp','gx','gy'}, use_global_device_ids=true, to_apply=%region_3.0 | all-reduce | flops 1 | bytes 8 | tf_op jit(solution)/shard_map/pmax | solution.py:146
  89.8 2.7 %collective-permute-start.3 = (f32[5,20,2,128]{3,2,1,0:T(2,128)S(1)}, f32[5,20,2,128]{3,2,1,0:T(2,128)S(1)}, u32[]{:S(2)}, u32[]{:S(2)}) collective-permute-start(f32[5,20,2,128]{3,2,1,0:T(2,128)S(1)} %get-tuple-element.219), channel_id=1, source_target_pairs={{16,0},{32,16},{48,32},{0,48},{17,1},{33,17},{49,33},{1,49},{18,2}... | collective-permute-start | bytes 307208 | tf_op jit(solution)/shard_map/ppermute | solution.py:22
  93.6 1.2 multiply_subtract_fusion.2
  94.9 1.8 fusion.26
  97.4 0.3 fusion.3
  97.8 1.0 scatter.50
  98.8 1.0 scatter.46
  99.8 2.6 %copy.41 = f32[5,20,20,2]{2,3,1,0:T(2,128)} copy(f32[5,20,20,2]{3,2,1,0:T(8,128)} %get-tuple-element.205) | data formatting | bytes 32000
  102.4 2.6 %copy.42 = f32[5,20,20,2]{2,3,1,0:T(2,128)} copy(f32[5,20,20,2]{3,2,1,0:T(8,128)} %get-tuple-element.206) | data formatting | bytes 32000
  105.0 1.8 collective-permute-start.5
  106.9 0.9 slice_bitcast_fusion.3
  108.1 0.9 copy-done.4
  109.0 0.3 copy-done.3
  109.4 1.3 multiply_subtract_fusion.1
  110.6 1.6 copy.37
  112.3 1.6 copy.38
  114.1 0.5 broadcast_divide_fusion
  115.1 0.4 slice_subtract_fusion
  115.5 0.4 minimum_add_fusion
  115.9 1.1 fusion.1
  117.4 0.3 slice_bitcast_fusion.1
  117.7 0.3 multiply_reduce_fusion
  118.1 0.8 multiply_subtract_fusion
  118.9 0.3 copy-done.1
  119.2 0.3 copy-done.2
  119.5 1.1 select_bitcast_fusion
  120.7 11.5 %all-gather = bf16[1,64,16,128]{3,2,0,1:T(8,128)(2,1)S(1)} all-gather(bf16[1,16,16,128]{3,2,0,1:T(8,128)(2,1)S(1)} %fusion.22), channel_id=2, replica_groups=mesh['grp'=4,'gx'=4,'gy'=16] {'grp'}, dimensions={1}, use_global_device_ids=true | all-gather | bytes 327680 | tf_op jit(solution)/shard_map/all_gather | solution.py:158
  132.3 2.7 %collective-permute-start.6 = (f32[16,3,8]{0,2,1:T(8,128)S(1)}, f32[16,3,8]{0,2,1:T(8,128)S(1)}, u32[]{:S(2)}, u32[]{:S(2)}) collective-permute-start(f32[16,3,8]{0,2,1:T(8,128)S(1)} %slice_select_fusion), channel_id=1, source_target_pairs={{0,8},{1,9},{2,10},{3,11},{4,12},{5,13},{6,14},{7,15},{8,0},{9,1},... | collective-permute-start | bytes 4616 | tf_op jit(solution)/shard_map/ppermute | solution.py:11
  135.2 28.1 %reshape.589 = bf16[24,2,8,2,64,2]{5,4,3,2,1,0:T(8,128)(2,1)} reshape(bf16[1,48,16,128]{3,2,0,1:T(8,128)(2,1)S(1)} %get-tuple-element.232) | data formatting | bytes 393216 | tf_op jit(solution)/shard_map/reshape | solution.py:118
  163.2 7.2 %reduce_max.66 = bf16[24,8,64]{2,1,0:T(8,128)(2,1)S(1)} reduce(bf16[24,2,8,2,64,2]{5,4,3,2,1,0:T(8,128)(2,1)} %reshape.589, bf16[]{:T(256)} %constant.340.clone.1), dimensions={1,3,5}, to_apply=%region_14.0 | reduce | flops 86016 | bytes 221186 | tf_op jit(solution)/shard_map/reduce_max | solution.py:117
  170.4 3.3 %reshape.590 = bf16[12,2,4,2,32,2]{5,4,3,2,1,0:T(8,128)(2,1)S(1)} reshape(bf16[24,8,64]{2,1,0:T(8,128)(2,1)S(1)} %reduce_max.66) | data formatting | bytes 49152 | tf_op jit(solution)/shard_map/reshape | solution.py:118
  173.8 0.4 reduce_max.80
  174.2 1.5 collective-permute-start.7
  175.8 0.6 select_bitcast_fusion.1
  176.4 1.7 reduce_max.82
  178.3 2.3 %collective-permute-start.8 = (f32[16,3,2]{0,2,1:T(2,128)S(1)}, f32[16,3,2]{0,2,1:T(2,128)S(1)}, u32[]{:S(2)}, u32[]{:S(2)}) collective-permute-start(f32[16,3,2]{0,2,1:T(2,128)S(1)} %broadcast_select_fusion.1), channel_id=1, source_target_pairs={{0,2},{1,3},{2,0},{3,1},{4,6},{5,7},{6,4},{7,5},{8,10},{9,11},{10,... | collective-permute-start | bytes 1160 | tf_op jit(solution)/shard_map/ppermute | solution.py:11
  180.6 0.3 reduce_max.83
  180.9 0.4 reduce_max.84
  181.9 6.3 %collective-permute-start.9 = (f32[16,3,1]{0,2,1:T(1,128)S(1)}, f32[16,3,1]{0,2,1:T(1,128)S(1)}, u32[]{:S(2)}, u32[]{:S(2)}) collective-permute-start(f32[16,3,1]{0,2,1:T(1,128)S(1)} %broadcast_select_fusion.2), channel_id=1, source_target_pairs={{0,1},{1,0},{2,3},{3,2},{4,5},{5,4},{6,7},{7,6},{8,9},{9,8},{10,11... | collective-permute-start | bytes 584 | tf_op jit(solution)/shard_map/ppermute | solution.py:11
  188.2 0.6 select_bitcast_fusion.2
  189.0 0.6 fusion.23
  (74 shorter events, 4.8 us)
Async XLA Ops:
  0.6 10.7 %copy-start = (f32[1,5,16,16,128]{4,3,2,1,0:T(8,128)S(1)}, f32[1,5,16,16,128]{4,3,2,1,0:T(8,128)}, u32[]{:S(2)}) copy-start(f32[1,5,16,16,128]{4,3,2,1,0:T(8,128)} %param.26) | copy-start | bytes 1966084
  1.7 87.9 %collective-permute-start = (f32[5,2,16,128]{3,2,1,0:T(8,128)S(1)}, f32[5,2,16,128]{3,2,1,0:T(8,128)S(1)}, u32[]{:S(2)}, u32[]{:S(2)}) collective-permute-start(f32[5,2,16,128]{3,2,1,0:T(8,128)S(1)} %get-tuple-element.229), channel_id=1, source_target_pairs={{0,64},{64,128},{128,192},{192,0},{1,65},{65,129},{129,193},{193,1... | collective-permute-start | bytes 245768 | tf_op jit(solution)/shard_map/ppermute | solution.py:21
  5.5 84.1 %collective-permute-start.1 = (f32[5,2,16,128]{3,2,1,0:T(8,128)S(1)}, f32[5,2,16,128]{3,2,1,0:T(8,128)S(1)}, u32[]{:S(2)}, u32[]{:S(2)}) collective-permute-start(f32[5,2,16,128]{3,2,1,0:T(8,128)S(1)} %get-tuple-element.230), channel_id=1, source_target_pairs={{64,0},{128,64},{192,128},{0,192},{65,1},{129,65},{193,129},{1,193... | collective-permute-start | bytes 245768 | tf_op jit(solution)/shard_map/ppermute | solution.py:22
  89.7 5.1 %collective-permute-start.2 = (f32[5,20,2,128]{3,2,1,0:T(2,128)S(1)}, f32[5,20,2,128]{3,2,1,0:T(2,128)S(1)}, u32[]{:S(2)}, u32[]{:S(2)}) collective-permute-start(f32[5,20,2,128]{3,2,1,0:T(2,128)S(1)} %get-tuple-element.218), channel_id=1, source_target_pairs={{0,16},{16,32},{32,48},{48,0},{1,17},{17,33},{33,49},{49,1},{2,18}... | collective-permute-start | bytes 307208 | tf_op jit(solution)/shard_map/ppermute | solution.py:21
  89.8 5.0 %collective-permute-start.3 = (f32[5,20,2,128]{3,2,1,0:T(2,128)S(1)}, f32[5,20,2,128]{3,2,1,0:T(2,128)S(1)}, u32[]{:S(2)}, u32[]{:S(2)}) collective-permute-start(f32[5,20,2,128]{3,2,1,0:T(2,128)S(1)} %get-tuple-element.219), channel_id=1, source_target_pairs={{16,0},{32,16},{48,32},{0,48},{17,1},{33,17},{49,33},{1,49},{18,2}... | collective-permute-start | bytes 307208 | tf_op jit(solution)/shard_map/ppermute | solution.py:22
  105.0 7.2 %collective-permute-start.5 = (f32[5,20,20,2]{2,3,1,0:T(2,128)}, f32[5,20,20,2]{2,3,1,0:T(2,128)}, u32[]{:S(2)}, u32[]{:S(2)}) collective-permute-start(f32[5,20,20,2]{2,3,1,0:T(2,128)} %copy.42), channel_id=1, source_target_pairs={{1,0},{2,1},{3,2},{4,3},{5,4},{6,5},{7,6},{8,7},{9,8},{10,9},{11,1... | collective-permute-start | bytes 48008 | tf_op jit(solution)/shard_map/ppermute | solution.py:22
  106.9 3.8 %collective-permute-start.4 = (f32[5,20,20,2]{2,3,1,0:T(2,128)}, f32[5,20,20,2]{2,3,1,0:T(2,128)}, u32[]{:S(2)}, u32[]{:S(2)}) collective-permute-start(f32[5,20,20,2]{2,3,1,0:T(2,128)} %copy.41), channel_id=1, source_target_pairs={{0,1},{1,2},{2,3},{3,4},{4,5},{5,6},{6,7},{7,8},{8,9},{9,10},{10,1... | collective-permute-start | bytes 48008 | tf_op jit(solution)/shard_map/ppermute | solution.py:21
  107.8 1.2 copy-start.4
  108.0 1.4 copy-start.3
  118.1 1.1 copy-start.1
  118.1 1.4 copy-start.2
  132.3 41.8 %collective-permute-start.6 = (f32[16,3,8]{0,2,1:T(8,128)S(1)}, f32[16,3,8]{0,2,1:T(8,128)S(1)}, u32[]{:S(2)}, u32[]{:S(2)}) collective-permute-start(f32[16,3,8]{0,2,1:T(8,128)S(1)} %slice_select_fusion), channel_id=1, source_target_pairs={{0,8},{1,9},{2,10},{3,11},{4,12},{5,13},{6,14},{7,15},{8,0},{9,1},... | collective-permute-start | bytes 4616 | tf_op jit(solution)/shard_map/ppermute | solution.py:11
  174.2 4.1 %collective-permute-start.7 = (f32[16,3,4]{0,2,1:T(4,128)S(1)}, f32[16,3,4]{0,2,1:T(4,128)S(1)}, u32[]{:S(2)}, u32[]{:S(2)}) collective-permute-start(f32[16,3,4]{0,2,1:T(4,128)S(1)} %slice_select_fusion.1), channel_id=1, source_target_pairs={{0,4},{1,5},{2,6},{3,7},{4,0},{5,1},{6,2},{7,3},{8,12},{9,13},{10,... | collective-permute-start | bytes 2312 | tf_op jit(solution)/shard_map/ppermute | solution.py:11
  178.3 3.5 %collective-permute-start.8 = (f32[16,3,2]{0,2,1:T(2,128)S(1)}, f32[16,3,2]{0,2,1:T(2,128)S(1)}, u32[]{:S(2)}, u32[]{:S(2)}) collective-permute-start(f32[16,3,2]{0,2,1:T(2,128)S(1)} %broadcast_select_fusion.1), channel_id=1, source_target_pairs={{0,2},{1,3},{2,0},{3,1},{4,6},{5,7},{6,4},{7,5},{8,10},{9,11},{10,... | collective-permute-start | bytes 1160 | tf_op jit(solution)/shard_map/ppermute | solution.py:11
  181.9 7.1 %collective-permute-start.9 = (f32[16,3,1]{0,2,1:T(1,128)S(1)}, f32[16,3,1]{0,2,1:T(1,128)S(1)}, u32[]{:S(2)}, u32[]{:S(2)}) collective-permute-start(f32[16,3,1]{0,2,1:T(1,128)S(1)} %broadcast_select_fusion.2), channel_id=1, source_target_pairs={{0,1},{1,0},{2,3},{3,2},{4,5},{5,4},{6,7},{7,6},{8,9},{9,8},{10,11... | collective-permute-start | bytes 584 | tf_op jit(solution)/shard_map/ppermute | solution.py:11
where the time goes:
time: 190 us
  blocking collectives  88.3 us (46%)
  local copies, waits for them, and re-layouts  50.4 us (27%)
  starting transfers between devices  24.4 us (13%)
  other arithmetic  24.1 us (13%)
    pmax x1, blocking collectives, body(): top_speed = lax.pmax(max_speed(fields), ('grp', 'gx', 'gy'))  76.8 us
    reshape x2, local copies, waits for them, and re-layouts, pool_once(): volume.reshape(num_planes // 2, 2, num_rows // 2, 2, num_cols // 2, 2)  31.4 us
    ppermute x4, starting transfers between devices, swapped(): lax.ppermute(shard, axis, [(i, i ^ 1 << distance) for i in range(lax.axis...  12.8 us
    all_gather x1, blocking collectives, body(): blocks = lax.all_gather(snapshot, 'grp', axis=0, tiled=True)  11.5 us
    reduce_max x7, other arithmetic, pool_once(): jnp.max(volume.reshape(num_planes // 2, 2, num_rows // 2, 2, num_cols //...  8.29 us
    ppermute x3, starting transfers between devices, padded_2(): after = lax.ppermute(first, axis, down)  7.62 us
    unnamed x12, local copies, waits for them, and re-layouts  7.13 us
    ppermute x3, starting transfers between devices, padded_2(): before = lax.ppermute(last, axis, up)  3.97 us
  transfers between devices with their start and end apart: 10, of which 2 were waited for; matrix products, arithmetic and copies ran while one was open for 28% of the time, Pallas kernels for 0%

commit v1 on v0

v1 whole, which is shorter than its diff:
```python
import jax
import jax.numpy as jnp
from jax import lax
from jax.experimental import pallas as pl
from jax.experimental.pallas import tpu as pltpu
from jax.sharding import PartitionSpec as P

F32 = jnp.float32
BF16 = jnp.bfloat16
MESH = pl.DeviceIdType.MESH

NF = 5
NZ = 16
NX = 16
NY = 128
N_GRP, N_GX, N_GY = 4, 4, 16
SLABS = 3
N_Z = 8
N_PLANE = 32
WZ = NZ + 4
WX = 32


def z_partner(k):
    g, x, y = lax.axis_index("grp"), lax.axis_index("gx"), lax.axis_index("gy")
    z = lax.rem(g * 2 + y // 8 + k, N_Z)
    return {"grp": z // 2, "gx": x, "gy": lax.rem(z, 2) * 8 + lax.rem(y, 8)}


def plane_partner(k):
    g, x, y = lax.axis_index("grp"), lax.axis_index("gx"), lax.axis_index("gy")
    i = lax.rem(x * 8 + lax.rem(y, 8) + k, N_PLANE)
    return {"grp": g, "gx": i // 8, "gy": (y // 8) * 8 + lax.rem(i, 8)}


def shifted(axis, step):
    place = {a: lax.axis_index(a) for a in ("grp", "gx", "gy")}
    count = {"grp": N_GRP, "gx": N_GX, "gy": N_GY}[axis]
    place[axis] = lax.rem(place[axis] + step + count, count)
    return place


def side(state, d):
    rho, p = state[0], state[4]
    v = state[1:4]
    m = [rho * a for a in v]
    energy = 2.5 * p + 0.5 * (m[0] * v[0] + m[1] * v[1] + m[2] * v[2])
    vd = state[d]
    fields = [rho, *m, energy]
    flux = [m[d - 1], m[0] * vd, m[1] * vd, m[2] * vd, (energy + p) * vd]
    flux[d] = flux[d] + p
    return fields, flux, jnp.abs(vd) + jnp.sqrt(1.4 * p / rho)


def face(q0, q1, q2, q3, d):
    low, up = [], []
    for a0, a1, a2, a3 in zip(q0, q1, q2, q3):
        a, b, c = a1 - a0, a2 - a1, a3 - a2
        left = jnp.maximum(jnp.minimum(a, b), jnp.minimum(jnp.maximum(a, b), 0.0))
        right = jnp.maximum(jnp.minimum(b, c), jnp.minimum(jnp.maximum(b, c), 0.0))
        low.append(a1 + 0.5 * left)
        up.append(a2 - 0.5 * right)
    ul, fl, rl = side(low, d)
    uu, fu, ru = side(up, d)
    wave = jnp.maximum(rl, ru)
    return [(a + b) - wave * (e - c) for a, b, c, e in zip(fl, fu, ul, uu)]


def kernel(
    state_ref, dir_ref, new_ref, view_ref, fine_ref, coarse_ref,
    S, W, CH, FX, FZ, NEW, SN, PK, GY, VT, LH, SO,
    send_z, send_x, send_y, recv_z, recv_x, recv_y,
    max0, max1, max1v, max2, recv_v, recv_o,
    in_sem, out_sem, hs_sem, hr_sem, ms_sem, mr_sem, vs_sem, vr_sem, os_sem, or_sem,
):
    g, gy = lax.axis_index("grp"), lax.axis_index("gy")
    is_viz = g == SLABS
    load = pltpu.make_async_copy(state_ref, S, in_sem)
    load.start()

    z_parts = [z_partner(k) for k in range(1, N_Z)]
    p_parts = [plane_partner(k) for k in range(1, N_PLANE)]
    y_up, y_down = shifted("gy", 1), shifted("gy", -1)
    barrier = pltpu.get_barrier_semaphore()
    greeted = z_parts + p_parts + [y_up, y_down]
    for part in greeted:
        pl.semaphore_signal(barrier, inc=1, device_id=part, device_id_type=MESH)

    lane = lax.broadcasted_iota(jnp.int32, (8, NY), 1)
    row16 = lax.broadcasted_iota(jnp.int32, (NX, NY), 0)
    lane16 = lax.broadcasted_iota(jnp.int32, (NX, NY), 1)
    W2 = W.reshape(NF * WZ * WX, NY)

    load.wait()

    def prims(z, carry):
        top, packed = carry[0], list(carry[1:])
        here = lax.shift_right_logical(lane, 2) == z
        for t in range(2):
            rows = slice(8 * t, 8 * t + 8)
            f = [S[0, i, z, rows, :] for i in range(NF)]
            inv = 1.0 / f[0]
            v = [a * inv for a in f[1:4]]
            p = 0.4 * (f[4] - 0.5 * (f[1] * v[0] + f[2] * v[1] + f[3] * v[2]))
            top = jnp.maximum(
                top,
                jnp.abs(v[0]) + jnp.abs(v[1]) + jnp.abs(v[2]) + 3.0 * jnp.sqrt(1.4 * p * inv),
            )
            for i, q in enumerate([f[0], *v, p]):
                W[i * WZ + 2 + z, 8 + 8 * t : 16 + 8 * t, :] = q
                packed[2 * i + t] = jnp.where(here, pltpu.roll(q, 4 * z + 2, 1), packed[2 * i + t])
        return (top, *packed)

    zero = jnp.zeros((8, NY), F32)
    carry = lax.fori_loop(0, NZ, prims, (zero,) + (zero,) * 10)
    max0[0] = jnp.max(carry[0], axis=0, keepdims=True)
    for i in range(NF):
        PK[i] = jnp.concatenate([carry[1 + 2 * i], carry[2 + 2 * i]], axis=0)
        send_y[i] = PK[i].astype(BF16)
        for r in range(2):
            send_z[0, i, r] = W[i * WZ + NZ + r, 8:24, :].astype(BF16)
            send_z[1, i, r] = W[i * WZ + 2 + r, 8:24, :].astype(BF16)
            for way, row in ((0, 22 + r), (1, 8 + r)):
                halves = [
                    W2[pl.ds((i * WZ + 2 + 8 * h) * WX + row, 8, stride=WX), :] for h in range(2)
                ]
                send_x[way, i, r] = jnp.concatenate(halves, axis=0).astype(BF16)

    pl.semaphore_wait(barrier, len(greeted))

    def remote(src, dst, ssem, rsem, part):
        return pltpu.make_async_remote_copy(
            src_ref=src, dst_ref=dst, send_sem=ssem, recv_sem=rsem, device_id=part, device_id_type=MESH
        )

    for k, part in enumerate(z_parts):
        remote(max0.at[0], max1.at[k], ms_sem.at[0], mr_sem.at[0], part).start()
    halo = []
    for way in range(2):
        step = 1 - 2 * way
        halo.append(
            remote(send_y, recv_y.at[way], hs_sem.at[way], hr_sem.at[way], (y_up, y_down)[way])
        )
    for way in range(2):
        step = 1 - 2 * way
        halo.append(
            remote(
                send_x.at[way], recv_x.at[way], hs_sem.at[2 + way], hr_sem.at[2 + way], shifted("gx", step)
            )
        )
    for way in range(2):
        step = 1 - 2 * way
        halo.append(
            remote(
                send_z.at[way], recv_z.at[way], hs_sem.at[4 + way], hr_sem.at[4 + way], shifted("grp", step)
            )
        )
    for copy in halo:
        copy.start()

    def z_face(p, _):
        for t in range(2):
            rows = slice(8 + 8 * t, 16 + 8 * t)
            q = [[W[i * WZ + p + j, rows, :] for i in range(NF)] for j in range(4)]
            for i, a in enumerate(face(*q, 1)):
                FZ[p, i, 8 * t : 8 * t + 8, :] = a
        return 0

    lax.fori_loop(2, NZ - 1, z_face, 0)

    halo[0].wait()
    halo[1].wait()
    for t in range(2):
        rows = slice(8 * t, 8 * t + 8)
        q = [[], [], [], []]
        for i in range(NF):
            mine = PK[i, rows, :]
            other = recv_y[1, i, :, :].astype(F32)[rows]
            q[0].append(mine)
            q[1].append(pltpu.roll(mine, NY - 1, 1))
            q[2].append(pltpu.roll(other, NY - 2, 1))
            q[3].append(pltpu.roll(other, NY - 3, 1))
        for i, a in enumerate(face(*q, 3)):
            GY[i, rows, :] = a

    def y_pass(z, _):
        for t in range(2):
            rows = slice(8 * t, 8 * t + 8)
            q = [[], [], [], []]
            for i in range(NF):
                own = W[i * WZ + 2 + z, 8 + 8 * t : 16 + 8 * t, :]
                low = pltpu.roll(recv_y[0, i, :, :].astype(F32)[rows], lax.rem(NY - 4 * z, NY), 1)
                high = pltpu.roll(recv_y[1, i, :, :].astype(F32)[rows], 125 - 4 * z, 1)
                q[0].append(jnp.where(lane < 2, low, pltpu.roll(own, 2, 1)))
                q[1].append(jnp.where(lane < 1, pltpu.roll(low, NY - 1, 1), pltpu.roll(own, 1, 1)))
                q[2].append(own)
                q[3].append(jnp.where(lane == NY - 1, high, pltpu.roll(own, NY - 1, 1)))
            for i, a in enumerate(face(*q, 3)):
                end = pltpu.roll(GY[i, rows, :], 127 - 4 * z, 1)
                above = jnp.where(lane == NY - 1, end, pltpu.roll(a, NY - 1, 1))
                CH[i, z, rows, :] = above - a
        return 0

    lax.fori_loop(0, NZ, y_pass, 0)

    def landed(dst, sem):
        remote(dst, dst, ms_sem.at[2], sem, y_up).wait_recv()

    def left(src, sem):
        remote(src, src, sem, mr_sem.at[2], y_up).wait_send()

    landed(max1, mr_sem.at[0])
    left(max1, ms_sem.at[0])
    top = max0[0]
    for k in range(N_Z - 1):
        top = jnp.maximum(top, max1[k])
    max1v[0] = top
    for k, part in enumerate(p_parts):
        remote(max1v.at[0], max2.at[k], ms_sem.at[1], mr_sem.at[1], part).start()

    halo[2].wait()
    halo[3].wait()
    for way, row in ((0, 6), (1, 24)):
        for i in range(NF):
            for r in range(2):
                rows = recv_x[way, i, r].astype(F32)
                for h in range(2):
                    W2[pl.ds((i * WZ + 2 + 8 * h) * WX + row + r, 8, stride=WX), :] = rows[8 * h : 8 * h + 8]
    FX2 = FX.reshape(NF * NZ * 24, NY)
    for h in range(2):
        q = [
            [W2[pl.ds((i * WZ + 2 + 8 * h) * WX + 22 + j, 8, stride=WX), :] for i in range(NF)]
            for j in range(4)
        ]
        for i, a in enumerate(face(*q, 2)):
            FX2[pl.ds((i * NZ + 8 * h) * 24 + 16, 8, stride=24), :] = a

    def x_pass(z, _):
        for t in range(2):
            q = [
                [W[i * WZ + 2 + z, 6 + j + 8 * t : 14 + j + 8 * t, :] for i in range(NF)] for j in range(4)
            ]
            for i, a in enumerate(face(*q, 2)):
                FX[i * NZ + z, 8 * t : 8 * t + 8, :] = a
        for t in range(2):
            rows = slice(8 * t, 8 * t + 8)
            for i in range(NF):
                CH[i, z, rows, :] = CH[i, z, rows, :] + (
                    FX[i * NZ + z, 8 * t + 1 : 8 * t + 9, :] - FX[i * NZ + z, rows, :]
                )
        return 0

    lax.fori_loop(0, NZ, x_pass, 0)

    halo[4].wait()
    halo[5].wait()
    for i in range(NF):
        for r in range(2):
            W[i * WZ + r, 8:24, :] = recv_z[0, i, r].astype(F32)
            W[i * WZ + 2 + NZ + r, 8:24, :] = recv_z[1, i, r].astype(F32)
    lax.fori_loop(0, 2, z_face, 0)
    lax.fori_loop(NZ - 1, NZ + 1, z_face, 0)

    def gather_change(z, _):
        for i in range(NF):
            CH[i, z] = CH[i, z] + (FZ[z + 1, i] - FZ[z, i])
        return 0

    lax.fori_loop(0, NZ, gather_change, 0)

    facing = jnp.zeros((NX, NY), jnp.int32)
    for x in range(NX):
        facing = jnp.where(row16 == x, dir_ref[x], facing)
    fraction = (gy * NY + lane16).astype(F32) / F32(NY * N_GY - 1)
    dim = jnp.where(facing == 0, jnp.exp(-fraction), jnp.exp(-(1.0 - fraction)))
    picks_from = lax.broadcasted_iota(jnp.int32, (NY, NY), 0)
    picks_to = lax.broadcasted_iota(jnp.int32, (NY, NY), 1)
    picks = (picks_from == 4 * picks_to) | (
        (picks_from == 16 * (picks_to - 32)) & (picks_to >= 32)
    )
    picks = picks.astype(F32).astype(BF16)

    landed(max2, mr_sem.at[1])
    left(max2, ms_sem.at[1])
    for k in range(N_PLANE - 1):
        top = jnp.maximum(top, max2[k])
    speed = jnp.max(top, axis=1, keepdims=True)
    half_step = jnp.broadcast_to(0.5 * (0.8 / speed), (8, NY))

    def lit(z, t):
        rows = slice(8 * t, 8 * t + 8)
        rho = S[0, 0, z, rows, :] - half_step * CH[0, z, rows, :]
        NEW[0, 0, z, rows, :] = rho
        snap = rho.astype(BF16).astype(F32)
        SN[z, rows, :] = snap
        return snap * dim[rows]

    def folded(z, bit, t):
        span = 8 << bit
        if bit == 3:
            a, b = lit(z, t), lit(z + 8, t)
        else:
            a, b = folded(z, bit + 1, t), folded(z + (1 << bit), bit + 1, t)
        a = jnp.maximum(a, pltpu.roll(a, NY - span, 1))
        b = jnp.maximum(b, pltpu.roll(b, span, 1))
        return jnp.where(lane & span == 0, a, b)

    halves = []
    for t in range(2):
        a = folded(0, 0, t)
        for span in (4, 2, 1):
            a = jnp.maximum(a, pltpu.roll(a, NY - span, 1))
        halves.append(a)
    VT[...] = jnp.transpose(jnp.concatenate(halves + [jnp.zeros((NY - NX, NY), F32)], axis=0))

    @pl.when(g < SLABS)
    def _():
        for k in range(N_GY):
            to = lax.rem(gy + k, N_GY)
            part = {"grp": SLABS, "gx": lax.axis_index("gx"), "gy": to}
            remote(
                VT.at[pl.ds(8 * to, 1)], recv_v.at[g * N_GY + gy], vs_sem, vr_sem, part
            ).start()

    tiles = []
    whole = None
    for zg in range(4):
        for t in range(2):
            rows = slice(8 * t, 8 * t + 8)
            m = SN[4 * zg, rows, :]
            for j in range(1, 4):
                m = jnp.maximum(m, SN[4 * zg + j, rows, :])
            for span in (1, 2):
                m = jnp.maximum(m, pltpu.roll(m, NY - span, 1))
            for span in (1, 2):
                m = jnp.maximum(m, pltpu.roll(m, 8 - span, 0))
            tiles.append(m)
            whole = m if whole is None else jnp.maximum(whole, m)
    for span in (4, 8):
        whole = jnp.maximum(whole, pltpu.roll(whole, NY - span, 1))
    whole = jnp.maximum(whole, pltpu.roll(whole, 4, 0))
    left_hand = jnp.concatenate(tiles + [whole, whole], axis=0).astype(BF16)
    LH[...] = jnp.dot(left_hand, picks, preferred_element_type=F32)
    rows = jnp.concatenate([LH[pl.ds(0, 8, stride=4), :], LH[pl.ds(32, 8, stride=4), :]], axis=0)
    last = jnp.broadcast_to(LH[64:65, :], (NX, NY))
    SO[...] = jnp.where(lane16 < 32, rows, last).astype(BF16)

    @pl.when(g < SLABS)
    def _():
        part = {"grp": SLABS, "gx": lax.axis_index("gx"), "gy": gy}
        remote(SO, recv_o.at[g], os_sem, or_sem, part).start()

    def update(z, _):
        for i in range(1, NF):
            for t in range(2):
                rows = slice(8 * t, 8 * t + 8)
                NEW[0, i, z, rows, :] = S[0, i, z, rows, :] - half_step * CH[i, z, rows, :]
        return 0

    lax.fori_loop(0, NZ, update, 0)

    view_ref[...] = jnp.zeros(view_ref.shape, F32)
    fine_ref[...] = jnp.zeros(fine_ref.shape, BF16)
    coarse_ref[...] = jnp.zeros(coarse_ref.shape, BF16)

    @pl.when(g < SLABS)
    def _():
        out = pltpu.make_async_copy(NEW, new_ref, out_sem)
        out.start()
        rows16 = recv_v.at[pl.ds(0, N_GY)]
        left(rows16, vs_sem)
        left(SO, os_sem)
        out.wait()

    @pl.when(is_viz)
    def _():
        out = pltpu.make_async_copy(S, new_ref, out_sem)
        out.start()
        landed(recv_o, or_sem)
        for s in range(SLABS):
            block = recv_o[s]
            for zg in range(4):
                fine_ref[0, 4 * s + zg] = block[4 * zg : 4 * zg + 4, :32]
            coarse_ref[0, s] = block[0:1, 32:40]
        landed(recv_v, vr_sem)
        rows = []
        for s in range(SLABS):
            a = recv_v[s * N_GY]
            for k in range(1, N_GY):
                a = jnp.maximum(a, recv_v[s * N_GY + k])
            rows.append(a)
        view = jnp.concatenate(rows, axis=0)
        for x in range(NX):
            view_ref[0, x] = view[:, x : x + 1]
        out.wait()


def body(state, view_dir):
    any_space = pl.BlockSpec(memory_space=pl.ANY)
    vmem = pl.BlockSpec(memory_space=pltpu.VMEM)
    dma = pltpu.SemaphoreType.DMA
    return pl.pallas_call(
        kernel,
        out_shape=(
            jax.ShapeDtypeStruct(state.shape, F32),
            jax.ShapeDtypeStruct((1, NX, SLABS, 1), F32),
            jax.ShapeDtypeStruct((1, 12, 4, 32), BF16),
            jax.ShapeDtypeStruct((1, 3, 1, 8), BF16),
        ),
        in_specs=[any_space, pl.BlockSpec(memory_space=pltpu.SMEM)],
        out_specs=(any_space, vmem, vmem, vmem),
        scratch_shapes=[
            pltpu.VMEM(state.shape, F32),
            pltpu.VMEM((NF * WZ, WX, NY), F32),
            pltpu.VMEM((NF, NZ, NX, NY), F32),
            pltpu.VMEM((NF * NZ, 24, NY), F32),
            pltpu.VMEM((NZ + 1, NF, NX, NY), F32),
            pltpu.VMEM(state.shape, F32),
            pltpu.VMEM((NZ, NX, NY), F32),
            pltpu.VMEM((NF, NX, NY), F32),
            pltpu.VMEM((NF, NX, NY), F32),
            pltpu.VMEM((NY, NY), F32),
            pltpu.VMEM((80, NY), F32),
            pltpu.VMEM((NX, NY), BF16),
            pltpu.VMEM((2, NF, 2, NX, NY), BF16),
            pltpu.VMEM((2, NF, 2, NZ, NY), BF16),
            pltpu.VMEM((NF, NX, NY), BF16),
            pltpu.VMEM((2, NF, 2, NX, NY), BF16),
            pltpu.VMEM((2, NF, 2, NZ, NY), BF16),
            pltpu.VMEM((2, NF, NX, NY), BF16),
            pltpu.VMEM((1, 1, NY), F32),
            pltpu.VMEM((N_Z - 1, 1, NY), F32),
            pltpu.VMEM((1, 1, NY), F32),
            pltpu.VMEM((N_PLANE - 1, 1, NY), F32),
            pltpu.VMEM((SLABS * N_GY, 1, NY), F32),
            pltpu.VMEM((SLABS, NX, NY), BF16),
            dma, dma, dma((6,)), dma((6,)), dma((3,)), dma((3,)), dma, dma, dma, dma,
        ],
        compiler_params=pltpu.CompilerParams(collective_id=0, has_side_effects=True),
    )(state, view_dir)


def solution(mesh):
    in_specs = (P("grp", None, None, "gx", "gy"), P("gx"))
    out_specs = (
        P("grp", None, None, "gx", "gy"),
        P("grp", "gx", None, "gy"),
        P("grp", None, "gx", "gy"),
        P("grp", None, "gx", "gy"),
    )
    return jax.shard_map(body, mesh=mesh, in_specs=in_specs, out_specs=out_specs, check_vma=False)
```

time: 190 us -> 32.4 us (0.17)
  blocking collectives: 88.3 us -> 0 us
  local copies, waits for them, and re-layouts: 50.4 us -> 5.23 us
  Pallas kernels: 0 us -> 26.3 us
  starting transfers between devices: 24.4 us -> 0 us
  other arithmetic: 24.1 us -> 0 us
    pmax x1 -> x0, blocking collectives: 76.8 us -> none  [body(): top_speed = lax.pmax(max_speed(fields), ('grp', 'gx', 'gy'))]
    reshape x2 -> x0, local copies, waits for them, and re-layouts: 31.4 us -> none  [pool_once(): volume.reshape(num_planes // 2, 2, num_rows // 2, 2, num_cols // 2, 2)]
    pallas_call x0 -> x1, Pallas kernels: none -> 26.3 us  [body(): pl.pallas_call(kernel, out_shape=(jax.ShapeDtypeStruct(state.shape, F32),...]
    ppermute x10 -> x0, starting transfers between devices: 24.4 us -> none  [the longest x4 12.8 us: swapped(): lax.ppermute(shard, axis, [(i, i ^ 1 << distance) for i in range(lax.axis...]
    all_gather x1 -> x0, blocking collectives: 11.5 us -> none  [body(): blocks = lax.all_gather(snapshot, 'grp', axis=0, tiled=True)]
    reduce_max x9 -> x0, other arithmetic: 9.13 us -> none  [the longest x7 8.29 us: pool_once(): jnp.max(volume.reshape(num_planes // 2, 2, num_rows // 2, 2, num_cols //...]
    unnamed x12 -> x6, local copies, waits for them, and re-layouts: 7.13 us -> 3.26 us
    sub x6 -> x0, other arithmetic: 3.81 us -> none  [the longest x3 3.22 us: divergence(): 0.5 * (physical_flux(lower_state, lower_fields, direction) + physical_flu...]
  transfers between devices with their start and end apart: 10 -> 0, of which waited for: 2 -> 0; matrix products, arithmetic and copies ran while one was open for 28% -> 0% of each run, Pallas kernels for 0% -> 0%
where the time goes in v1:
time: 32.4 us; the launch traced here: 32.2 us
  Pallas kernels  26.3 us (81%)
  local copies, waits for them, and re-layouts  5.23 us (16%)
  between operations  0.65 us (2%)
    pallas_call x1, Pallas kernels, body(): pl.pallas_call(kernel, out_shape=(jax.ShapeDtypeStruct(state.shape, F32),...  26.3 us
    unnamed x6, local copies, waits for them, and re-layouts  3.26 us
    pallas_call x2, local copies, waits for them, and re-layouts, body(): pl.pallas_call(kernel, out_shape=(jax.ShapeDtypeStruct(state.shape, F32),...  1.97 us

profile of v1, /device:TPU:1, one launch (start us, length us, event | category | flops | bytes accessed | tf_op | source)
XLA Modules:
  0.0 32.2 jit_solution(12371057006974317539)
XLA Ops:
  0.6 26.3 %shard_map.57 = (f32[1,5,16,16,128]{4,3,2,1,0:T(8,128)}, f32[1,16,3,1]{3,2,1,0:T(4,128)}, bf16[1,12,4,32]{3,2,1,0:T(4,128)(2,1)}, bf16[1,3,1,8]{3,2,1,0:T(2,128)(2,1)}) custom-call(f32[1,5,16,16,128]{4,3,2,1,0:T(8,128)} %state_ref.1, s32[16]{0:T(128)} %dir_ref.1), custom_call_target="tpu_custom_call" | custom-call | tf_op jit(solution)/shard_map/pallas_call | solution.py:402
  27.0 0.0 copy-start.1
  27.0 0.7 %copy-done.1 = bf16[1,3,1,8]{3,2,1,0:T(2,128)(2,1)S(1)} copy-done((bf16[1,3,1,8]{3,2,1,0:T(2,128)(2,1)S(1)}, bf16[1,3,1,8]{3,2,1,0:T(2,128)(2,1)}, u32[]{:S(2)}) %copy-start.1) | copy-done | bytes 72
  27.6 0.6 %copy.7 = bf16[1,3,1,8]{3,1,2,0:T(4,128)(2,1)} copy(bf16[1,3,1,8]{3,2,1,0:T(2,128)(2,1)S(1)} %copy-done.1) | data formatting | bytes 96 | tf_op jit(solution)/shard_map/pallas_call | solution.py:402
  28.2 1.4 %copy.6 = f32[1,16,3,1]{1,3,2,0:T(1,128)} copy(f32[1,16,3,1]{3,2,1,0:T(4,128)} %get-tuple-element.5) | data formatting | bytes 384 | tf_op jit(solution)/shard_map/pallas_call | solution.py:402
  29.6 0.0 copy-start
  29.6 2.0 %copy.10 = f32[1,5,16,16,128]{4,3,2,1,0:T(8,128)} copy(f32[1,5,16,16,128]{4,3,2,1,0:T(8,128)} %get-tuple-element.12) | data formatting | bytes 1310720
  31.6 0.0 copy-done
  31.6 0.6 %copy.11 = bf16[1,12,4,32]{3,2,1,0:T(4,128)(2,1)} copy(bf16[1,12,4,32]{3,2,1,0:T(4,128)(2,1)S(1)} %copy-done) | data formatting | bytes 6144
Async XLA Ops:
  27.0 0.7 %copy-start.1 = (bf16[1,3,1,8]{3,2,1,0:T(2,128)(2,1)S(1)}, bf16[1,3,1,8]{3,2,1,0:T(2,128)(2,1)}, u32[]{:S(2)}) copy-start(bf16[1,3,1,8]{3,2,1,0:T(2,128)(2,1)} %get-tuple-element.7) | copy-start | bytes 148
  29.6 2.0 %copy-start = (bf16[1,12,4,32]{3,2,1,0:T(4,128)(2,1)S(1)}, bf16[1,12,4,32]{3,2,1,0:T(4,128)(2,1)}, u32[]{:S(2)}) copy-start(bf16[1,12,4,32]{3,2,1,0:T(4,128)(2,1)} %get-tuple-element.14) | copy-start | bytes 9220

commit v2 on v1

--- a/solution.py
+++ b/solution.py
@@ -15,22 +15,23 @@
 NY = 128
 N_GRP, N_GX, N_GY = 4, 4, 16
 SLABS = 3
-N_Z = 8
-N_PLANE = 32
+N_NEAR = 16
+CHUNKS = 4
 WZ = NZ + 4
 WX = 32
 
 
-def z_partner(k):
+def near_devices():
     g, x, y = lax.axis_index("grp"), lax.axis_index("gx"), lax.axis_index("gy")
-    z = lax.rem(g * 2 + y // 8 + k, N_Z)
-    return {"grp": z // 2, "gx": x, "gy": lax.rem(z, 2) * 8 + lax.rem(y, 8)}
-
-
-def plane_partner(k):
-    g, x, y = lax.axis_index("grp"), lax.axis_index("gx"), lax.axis_index("gy")
-    i = lax.rem(x * 8 + lax.rem(y, 8) + k, N_PLANE)
-    return {"grp": g, "gx": i // 8, "gy": (y // 8) * 8 + lax.rem(i, 8)}
+    grps = [lax.rem(g + k, N_GRP) for k in range(N_GRP)]
+    gxs = [lax.rem(x + k, N_GX) for k in range(N_GX)]
+    other_core = y + 1 - 2 * lax.rem(y, 2)
+    cores = [y, other_core, lax.rem(y + 8, N_GY), lax.rem(other_core + 8, N_GY)]
+    in_plane = lax.rem(y, 8)
+    ys = [y - in_plane + lax.rem(in_plane + 2 * k, 8) for k in range(4)]
+    column = [{"grp": a, "gx": x, "gy": b} for a in grps for b in cores]
+    plane = [{"grp": g, "gx": a, "gy": b} for a in gxs for b in ys]
+    return column[1:], plane[1:]
 
 
 def shifted(axis, step):
@@ -67,19 +68,28 @@
 
 
 def kernel(
-    state_ref, dir_ref, new_ref, view_ref, fine_ref, coarse_ref,
-    S, W, CH, FX, FZ, NEW, SN, PK, GY, VT, LH, SO,
+    state_ref, dir_ref, NEW, view_ref, fine_ref, coarse_ref,
+    S, W, CH, FX, FZ, SN, PK, GY, VT, LH, SO,
     send_z, send_x, send_y, recv_z, recv_x, recv_y,
     max0, max1, max1v, max2, recv_v, recv_o,
     in_sem, out_sem, hs_sem, hr_sem, ms_sem, mr_sem, vs_sem, vr_sem, os_sem, or_sem,
 ):
     g, gy = lax.axis_index("grp"), lax.axis_index("gy")
     is_viz = g == SLABS
-    load = pltpu.make_async_copy(state_ref, S, in_sem)
-    load.start()
-
-    z_parts = [z_partner(k) for k in range(1, N_Z)]
-    p_parts = [plane_partner(k) for k in range(1, N_PLANE)]
+    depth = NZ // CHUNKS
+    loads = []
+    for n in range(CHUNKS):
+        planes = pl.ds(n * depth, depth)
+        loads.append(
+            pltpu.make_async_copy(state_ref.at[:, :, planes], S.at[:, :, planes], in_sem.at[n])
+        )
+        loads[-1].start()
+
+    @pl.when(is_viz)
+    def _():
+        pltpu.make_async_copy(state_ref, NEW, out_sem).start()
+
+    z_parts, p_parts = near_devices()
     y_up, y_down = shifted("gy", 1), shifted("gy", -1)
     barrier = pltpu.get_barrier_semaphore()
     greeted = z_parts + p_parts + [y_up, y_down]
@@ -91,7 +101,6 @@
     lane16 = lax.broadcasted_iota(jnp.int32, (NX, NY), 1)
     W2 = W.reshape(NF * WZ * WX, NY)
 
-    load.wait()
 
     def prims(z, carry):
         top, packed = carry[0], list(carry[1:])
@@ -112,8 +121,20 @@
         return (top, *packed)
 
     zero = jnp.zeros((8, NY), F32)
-    carry = lax.fori_loop(0, NZ, prims, (zero,) + (zero,) * 10)
+    carry = (zero,) * 11
+    for n in range(CHUNKS):
+        loads[n].wait()
+        carry = lax.fori_loop(n * depth, (n + 1) * depth, prims, carry)
     max0[0] = jnp.max(carry[0], axis=0, keepdims=True)
+    pl.semaphore_wait(barrier, len(greeted))
+
+    def remote(src, dst, ssem, rsem, part):
+        return pltpu.make_async_remote_copy(
+            src_ref=src, dst_ref=dst, send_sem=ssem, recv_sem=rsem, device_id=part, device_id_type=MESH
+        )
+
+    for k, part in enumerate(z_parts):
+        remote(max0.at[0], max1.at[k], ms_sem.at[0], mr_sem.at[0], part).start()
     for i in range(NF):
         PK[i] = jnp.concatenate([carry[1 + 2 * i], carry[2 + 2 * i]], axis=0)
         send_y[i] = PK[i].astype(BF16)
@@ -126,15 +147,6 @@
                 ]
                 send_x[way, i, r] = jnp.concatenate(halves, axis=0).astype(BF16)
 
-    pl.semaphore_wait(barrier, len(greeted))
-
-    def remote(src, dst, ssem, rsem, part):
-        return pltpu.make_async_remote_copy(
-            src_ref=src, dst_ref=dst, send_sem=ssem, recv_sem=rsem, device_id=part, device_id_type=MESH
-        )
-
-    for k, part in enumerate(z_parts):
-        remote(max0.at[0], max1.at[k], ms_sem.at[0], mr_sem.at[0], part).start()
     halo = []
     for way in range(2):
         step = 1 - 2 * way
@@ -167,56 +179,6 @@
         return 0
 
     lax.fori_loop(2, NZ - 1, z_face, 0)
-
-    halo[0].wait()
-    halo[1].wait()
-    for t in range(2):
-        rows = slice(8 * t, 8 * t + 8)
-        q = [[], [], [], []]
-        for i in range(NF):
-            mine = PK[i, rows, :]
-            other = recv_y[1, i, :, :].astype(F32)[rows]
-            q[0].append(mine)
-            q[1].append(pltpu.roll(mine, NY - 1, 1))
-            q[2].append(pltpu.roll(other, NY - 2, 1))
-            q[3].append(pltpu.roll(other, NY - 3, 1))
-        for i, a in enumerate(face(*q, 3)):
-            GY[i, rows, :] = a
-
-    def y_pass(z, _):
-        for t in range(2):
-            rows = slice(8 * t, 8 * t + 8)
-            q = [[], [], [], []]
-            for i in range(NF):
-                own = W[i * WZ + 2 + z, 8 + 8 * t : 16 + 8 * t, :]
-                low = pltpu.roll(recv_y[0, i, :, :].astype(F32)[rows], lax.rem(NY - 4 * z, NY), 1)
-                high = pltpu.roll(recv_y[1, i, :, :].astype(F32)[rows], 125 - 4 * z, 1)
-                q[0].append(jnp.where(lane < 2, low, pltpu.roll(own, 2, 1)))
-                q[1].append(jnp.where(lane < 1, pltpu.roll(low, NY - 1, 1), pltpu.roll(own, 1, 1)))
-                q[2].append(own)
-                q[3].append(jnp.where(lane == NY - 1, high, pltpu.roll(own, NY - 1, 1)))
-            for i, a in enumerate(face(*q, 3)):
-                end = pltpu.roll(GY[i, rows, :], 127 - 4 * z, 1)
-                above = jnp.where(lane == NY - 1, end, pltpu.roll(a, NY - 1, 1))
-                CH[i, z, rows, :] = above - a
-        return 0
-
-    lax.fori_loop(0, NZ, y_pass, 0)
-
-    def landed(dst, sem):
-        remote(dst, dst, ms_sem.at[2], sem, y_up).wait_recv()
-
-    def left(src, sem):
-        remote(src, src, sem, mr_sem.at[2], y_up).wait_send()
-
-    landed(max1, mr_sem.at[0])
-    left(max1, ms_sem.at[0])
-    top = max0[0]
-    for k in range(N_Z - 1):
-        top = jnp.maximum(top, max1[k])
-    max1v[0] = top
-    for k, part in enumerate(p_parts):
-        remote(max1v.at[0], max2.at[k], ms_sem.at[1], mr_sem.at[1], part).start()
 
     halo[2].wait()
     halo[3].wait()
@@ -245,12 +207,62 @@
         for t in range(2):
             rows = slice(8 * t, 8 * t + 8)
             for i in range(NF):
-                CH[i, z, rows, :] = CH[i, z, rows, :] + (
+                CH[i, z, rows, :] = (
                     FX[i * NZ + z, 8 * t + 1 : 8 * t + 9, :] - FX[i * NZ + z, rows, :]
                 )
         return 0
 
     lax.fori_loop(0, NZ, x_pass, 0)
+
+    def landed(dst, sem):
+        remote(dst, dst, ms_sem.at[2], sem, y_up).wait_recv()
+
+    def left(src, sem):
+        remote(src, src, sem, mr_sem.at[2], y_up).wait_send()
+
+    landed(max1, mr_sem.at[0])
+    left(max1, ms_sem.at[0])
+    top = max0[0]
+    for k in range(N_NEAR - 1):
+        top = jnp.maximum(top, max1[k])
+    max1v[0] = top
+    for k, part in enumerate(p_parts):
+        remote(max1v.at[0], max2.at[k], ms_sem.at[1], mr_sem.at[1], part).start()
+
+    halo[0].wait()
+    halo[1].wait()
+    for t in range(2):
+        rows = slice(8 * t, 8 * t + 8)
+        q = [[], [], [], []]
+        for i in range(NF):
+            mine = PK[i, rows, :]
+            other = recv_y[1, i, :, :].astype(F32)[rows]
+            q[0].append(mine)
+            q[1].append(pltpu.roll(mine, NY - 1, 1))
+            q[2].append(pltpu.roll(other, NY - 2, 1))
+            q[3].append(pltpu.roll(other, NY - 3, 1))
+        for i, a in enumerate(face(*q, 3)):
+            GY[i, rows, :] = a
+
+    def y_pass(z, _):
+        for t in range(2):
+            rows = slice(8 * t, 8 * t + 8)
+            q = [[], [], [], []]
+            for i in range(NF):
+                own = W[i * WZ + 2 + z, 8 + 8 * t : 16 + 8 * t, :]
+                low = pltpu.roll(recv_y[0, i, :, :].astype(F32)[rows], lax.rem(NY - 4 * z, NY), 1)
+                high = pltpu.roll(recv_y[1, i, :, :].astype(F32)[rows], 125 - 4 * z, 1)
+                q[0].append(jnp.where(lane < 2, low, pltpu.roll(own, 2, 1)))
+                q[1].append(jnp.where(lane < 1, pltpu.roll(low, NY - 1, 1), pltpu.roll(own, 1, 1)))
+                q[2].append(own)
+                q[3].append(jnp.where(lane == NY - 1, high, pltpu.roll(own, NY - 1, 1)))
+            for i, a in enumerate(face(*q, 3)):
+                end = pltpu.roll(GY[i, rows, :], 127 - 4 * z, 1)
+                above = jnp.where(lane == NY - 1, end, pltpu.roll(a, NY - 1, 1))
+                CH[i, z, rows, :] = CH[i, z, rows, :] + (above - a)
+        return 0
+
+    lax.fori_loop(0, NZ, y_pass, 0)
 
     halo[4].wait()
     halo[5].wait()
@@ -282,7 +294,7 @@
 
     landed(max2, mr_sem.at[1])
     left(max2, ms_sem.at[1])
-    for k in range(N_PLANE - 1):
+    for k in range(N_NEAR - 1):
         top = jnp.maximum(top, max2[k])
     speed = jnp.max(top, axis=1, keepdims=True)
     half_step = jnp.broadcast_to(0.5 * (0.8 / speed), (8, NY))
@@ -290,7 +302,6 @@
     def lit(z, t):
         rows = slice(8 * t, 8 * t + 8)
         rho = S[0, 0, z, rows, :] - half_step * CH[0, z, rows, :]
-        NEW[0, 0, z, rows, :] = rho
         snap = rho.astype(BF16).astype(F32)
         SN[z, rows, :] = snap
         return snap * dim[rows]
@@ -351,72 +362,70 @@
         remote(SO, recv_o.at[g], os_sem, or_sem, part).start()
 
     def update(z, _):
-        for i in range(1, NF):
+        for i in range(NF):
             for t in range(2):
                 rows = slice(8 * t, 8 * t + 8)
                 NEW[0, i, z, rows, :] = S[0, i, z, rows, :] - half_step * CH[i, z, rows, :]
         return 0
 
-    lax.fori_loop(0, NZ, update, 0)
-
     view_ref[...] = jnp.zeros(view_ref.shape, F32)
     fine_ref[...] = jnp.zeros(fine_ref.shape, BF16)
     coarse_ref[...] = jnp.zeros(coarse_ref.shape, BF16)
 
     @pl.when(g < SLABS)
     def _():
-        out = pltpu.make_async_copy(NEW, new_ref, out_sem)
-        out.start()
+        lax.fori_loop(0, NZ, update, 0)
         rows16 = recv_v.at[pl.ds(0, N_GY)]
         left(rows16, vs_sem)
         left(SO, os_sem)
-        out.wait()
 
     @pl.when(is_viz)
     def _():
-        out = pltpu.make_async_copy(S, new_ref, out_sem)
-        out.start()
         landed(recv_o, or_sem)
         for s in range(SLABS):
             block = recv_o[s]
             for zg in range(4):
                 fine_ref[0, 4 * s + zg] = block[4 * zg : 4 * zg + 4, :32]
-            coarse_ref[0, s] = block[0:1, 32:40]
+            coarse_ref[0, 0, s : s + 1, :] = block[0:1, 32:40]
         landed(recv_v, vr_sem)
-        rows = []
         for s in range(SLABS):
             a = recv_v[s * N_GY]
             for k in range(1, N_GY):
                 a = jnp.maximum(a, recv_v[s * N_GY + k])
-            rows.append(a)
-        view = jnp.concatenate(rows, axis=0)
-        for x in range(NX):
-            view_ref[0, x] = view[:, x : x + 1]
-        out.wait()
+            view_ref[0, s] = a[:, :NX]
+        pltpu.make_async_copy(state_ref, NEW, out_sem).wait()
+
+
+def put_out(new_in, view_in, fine_in, coarse_in, new_out, view_out, fine_out, coarse_out, sems):
+    copies = [
+        pltpu.make_async_copy(a, b, sems.at[n])
+        for n, (a, b) in enumerate(
+            ((new_in, new_out), (view_in, view_out), (fine_in, fine_out), (coarse_in, coarse_out))
+        )
+    ]
+    for copy in copies:
+        copy.start()
+    for copy in copies:
+        copy.wait()
 
 
 def body(state, view_dir):
     any_space = pl.BlockSpec(memory_space=pl.ANY)
     vmem = pl.BlockSpec(memory_space=pltpu.VMEM)
     dma = pltpu.SemaphoreType.DMA
-    return pl.pallas_call(
+    shapes = ((state.shape, F32), ((1, SLABS, 1, NX), F32), ((1, 12, 4, 32), BF16), ((1, 1, 3, 8), BF16))
+    new_state, view, fine, coarse = pl.pallas_call(
         kernel,
-        out_shape=(
-            jax.ShapeDtypeStruct(state.shape, F32),
-            jax.ShapeDtypeStruct((1, NX, SLABS, 1), F32),
-            jax.ShapeDtypeStruct((1, 12, 4, 32), BF16),
-            jax.ShapeDtypeStruct((1, 3, 1, 8), BF16),
-        ),
+        out_shape=tuple(pltpu.VMEM(*s) for s in shapes),
         in_specs=[any_space, pl.BlockSpec(memory_space=pltpu.SMEM)],
-        out_specs=(any_space, vmem, vmem, vmem),
+        out_specs=(vmem,) * 4,
         scratch_shapes=[
             pltpu.VMEM(state.shape, F32),
             pltpu.VMEM((NF * WZ, WX, NY), F32),
             pltpu.VMEM((NF, NZ, NX, NY), F32),
             pltpu.VMEM((NF * NZ, 24, NY), F32),
             pltpu.VMEM((NZ + 1, NF, NX, NY), F32),
-            pltpu.VMEM(state.shape, F32),
-            pltpu.VMEM((NZ, NX, NY), F32),
+                pltpu.VMEM((NZ, NX, NY), F32),
             pltpu.VMEM((NF, NX, NY), F32),
             pltpu.VMEM((NF, NX, NY), F32),
             pltpu.VMEM((NY, NY), F32),
@@ -429,15 +438,23 @@
             pltpu.VMEM((2, NF, 2, NZ, NY), BF16),
             pltpu.VMEM((2, NF, NX, NY), BF16),
             pltpu.VMEM((1, 1, NY), F32),
-            pltpu.VMEM((N_Z - 1, 1, NY), F32),
+            pltpu.VMEM((N_NEAR - 1, 1, NY), F32),
             pltpu.VMEM((1, 1, NY), F32),
-            pltpu.VMEM((N_PLANE - 1, 1, NY), F32),
+            pltpu.VMEM((N_NEAR - 1, 1, NY), F32),
             pltpu.VMEM((SLABS * N_GY, 1, NY), F32),
             pltpu.VMEM((SLABS, NX, NY), BF16),
-            dma, dma, dma((6,)), dma((6,)), dma((3,)), dma((3,)), dma, dma, dma, dma,
+            dma((CHUNKS,)), dma, dma((6,)), dma((6,)), dma((3,)), dma((3,)), dma, dma, dma, dma,
         ],
         compiler_params=pltpu.CompilerParams(collective_id=0, has_side_effects=True),
     )(state, view_dir)
+    new_state, view, fine, coarse = pl.pallas_call(
+        put_out,
+        out_shape=tuple(jax.ShapeDtypeStruct(*s) for s in shapes),
+        in_specs=[vmem] * 4,
+        out_specs=(any_space,) * 4,
+        scratch_shapes=[dma((4,))],
+    )(*(pltpu.with_memory_space_constraint(a, pltpu.VMEM) for a in (new_state, view, fine, coarse)))
+    return new_state, jnp.transpose(view, (0, 3, 1, 2)), fine, jnp.transpose(coarse, (0, 2, 1, 3))
 
 
 def solution(mesh):

time: 32.4 us -> 25.1 us (0.77)
  local copies, waits for them, and re-layouts: 5.23 us -> 0 us
  Pallas kernels: 26.3 us -> 24.4 us
    unnamed x6 -> x0, local copies, waits for them, and re-layouts: 3.26 us -> none
    pallas_call x2 -> x0, local copies, waits for them, and re-layouts: 1.97 us -> none  [body(): pl.pallas_call(kernel, out_shape=(jax.ShapeDtypeStruct(state.shape, F32),...]
    pallas_call x1 -> x2, Pallas kernels: 26.3 us -> 24.4 us  [the longest x1 23.5 us: body(): pl.pallas_call(kernel, out_shape=tuple((pltpu.VMEM(*s) for s in shapes)),...]
where the time goes in v2:
time: 25.1 us; the launch traced here: 25 us
  Pallas kernels  24.4 us (97%)
  between operations  0.64 us (3%)
    pallas_call x1, Pallas kernels, body(): pl.pallas_call(kernel, out_shape=tuple((pltpu.VMEM(*s) for s in shapes)),...  23.5 us
    pallas_call x1, Pallas kernels, body(): pl.pallas_call(put_out, out_shape=tuple((jax.ShapeDtypeStruct(*s) for s i...  0.88 us

profile of v2, /device:TPU:1, one launch (start us, length us, event | category | flops | bytes accessed | tf_op | source)
XLA Modules:
  0.0 25.0 jit_solution(6101582250801686268)
XLA Ops:
  0.6 23.5 %shard_map.57 = (f32[1,5,16,16,128]{4,3,2,1,0:T(8,128)S(1)}, f32[1,3,1,16]{3,2,1,0:T(1,128)S(1)}, bf16[1,12,4,32]{3,2,1,0:T(4,128)(2,1)S(1)}, bf16[1,1,3,8]{3,2,1,0:T(4,128)(2,1)S(1)}) custom-call(f32[1,5,16,16,128]{4,3,2,1,0:T(8,128)} %state_ref.1, s32[16]{0:T(128)} %dir_ref.1), custom_call_target="tpu_custom_call" | custom-call | tf_op jit(solution)/shard_map/pallas_call | solution.py:417
  24.1 0.9 %shard_map.58 = (f32[1,5,16,16,128]{4,3,2,1,0:T(8,128)}, f32[1,3,1,16]{3,2,1,0:T(1,128)}, bf16[1,12,4,32]{3,2,1,0:T(4,128)(2,1)}, bf16[1,1,3,8]{3,2,1,0:T(4,128)(2,1)}) custom-call(f32[1,5,16,16,128]{4,3,2,1,0:T(8,128)S(1)} %get-tuple-element.12.new_in, f32[1,3,1,16]{3,2,1,0:T(1,128)S(1)} %get-tuple-element.13.view_in, ...), custom_call_target="tpu_custom_call" | custom-call | tf_op jit(solution)/shard_map/pallas_call | solution.py:450

commit v3 on v2

--- a/solution.py
+++ b/solution.py
@@ -29,9 +29,10 @@
     cores = [y, other_core, lax.rem(y + 8, N_GY), lax.rem(other_core + 8, N_GY)]
     in_plane = lax.rem(y, 8)
     ys = [y - in_plane + lax.rem(in_plane + 2 * k, 8) for k in range(4)]
-    column = [{"grp": a, "gx": x, "gy": b} for a in grps for b in cores]
-    plane = [{"grp": g, "gx": a, "gy": b} for a in gxs for b in ys]
-    return column[1:], plane[1:]
+    far_first = (2, 1, 3, 0)
+    column = [{"grp": grps[k], "gx": x, "gy": b} for k in far_first for b in reversed(cores)]
+    plane = [{"grp": g, "gx": gxs[k], "gy": ys[j]} for k in far_first for j in far_first]
+    return column[:-1], plane[:-1]
 
 
 def shifted(axis, step):
@@ -69,7 +70,7 @@
 
 def kernel(
     state_ref, dir_ref, NEW, view_ref, fine_ref, coarse_ref,
-    S, W, CH, FX, FZ, SN, PK, GY, VT, LH, SO,
+    S, W, CH, FX, FZ, QY, SN, PK, GY, VT, LH, SO,
     send_z, send_x, send_y, recv_z, recv_x, recv_y,
     max0, max1, max1v, max2, recv_v, recv_o,
     in_sem, out_sem, hs_sem, hr_sem, ms_sem, mr_sem, vs_sem, vr_sem, os_sem, or_sem,
@@ -92,7 +93,7 @@
     z_parts, p_parts = near_devices()
     y_up, y_down = shifted("gy", 1), shifted("gy", -1)
     barrier = pltpu.get_barrier_semaphore()
-    greeted = z_parts + p_parts + [y_up, y_down]
+    greeted = z_parts[:8] + p_parts[:8] + [y_up, y_down] + z_parts[8:] + p_parts[8:]
     for part in greeted:
         pl.semaphore_signal(barrier, inc=1, device_id=part, device_id_type=MESH)
 
@@ -104,7 +105,7 @@
 
     def prims(z, carry):
         top, packed = carry[0], list(carry[1:])
-        here = lax.shift_right_logical(lane, 2) == z
+        here = lax.shift_right_logical(lane, 3) == z
         for t in range(2):
             rows = slice(8 * t, 8 * t + 8)
             f = [S[0, i, z, rows, :] for i in range(NF)]
@@ -117,7 +118,11 @@
             )
             for i, q in enumerate([f[0], *v, p]):
                 W[i * WZ + 2 + z, 8 + 8 * t : 16 + 8 * t, :] = q
-                packed[2 * i + t] = jnp.where(here, pltpu.roll(q, 4 * z + 2, 1), packed[2 * i + t])
+                packed[2 * i + t] = jnp.where(
+                    here, pltpu.roll(q, lax.rem(8 * z + 4, NY), 1), packed[2 * i + t]
+                )
+                for j, turn in enumerate((2, 1, NY - 1)):
+                    QY[j, i * NZ + z, rows, :] = pltpu.roll(q, turn, 1)
         return (top, *packed)
 
     zero = jnp.zeros((8, NY), F32)
@@ -179,6 +184,64 @@
         return 0
 
     lax.fori_loop(2, NZ - 1, z_face, 0)
+
+    def y_face(z, _):
+        for t in range(2):
+            rows = slice(8 * t, 8 * t + 8)
+            q = [[QY[j, i * NZ + z, rows, :] for i in range(NF)] for j in range(3)]
+            own = [W[i * WZ + 2 + z, 8 + 8 * t : 16 + 8 * t, :] for i in range(NF)]
+            for i, a in enumerate(face(q[0], q[1], own, q[2], 3)):
+                CH[i, z, rows, :] = a
+        return 0
+
+    lax.fori_loop(0, NZ, y_face, 0)
+
+    halo[0].wait()
+    halo[1].wait()
+    slot = lane & 7
+    for t in range(2):
+        rows = slice(8 * t, 8 * t + 8)
+        q = [[], [], [], []]
+        for i in range(NF):
+            own = PK[i, rows, :]
+            low = recv_y[0, i].astype(F32)[rows]
+            high = recv_y[1, i].astype(F32)[rows]
+            back = pltpu.roll(own, NY - 1, 1)
+            q[0].append(
+                jnp.where(
+                    slot == 2, own, jnp.where(slot == 3, pltpu.roll(own, 2, 1), pltpu.roll(low, 2, 1))
+                )
+            )
+            q[1].append(
+                jnp.where(
+                    slot == 2, back, jnp.where(slot == 4, pltpu.roll(low, 1, 1), pltpu.roll(own, 1, 1))
+                )
+            )
+            q[2].append(jnp.where(slot == 2, pltpu.roll(high, NY - 2, 1), own))
+            q[3].append(
+                jnp.where(
+                    slot == 2,
+                    pltpu.roll(high, NY - 3, 1),
+                    jnp.where(slot == 3, pltpu.roll(high, NY - 1, 1), back),
+                )
+            )
+        for i, a in enumerate(face(*q, 3)):
+            GY[i, rows, :] = a
+
+    def landed(dst, sem):
+        remote(dst, dst, ms_sem.at[2], sem, y_up).wait_recv()
+
+    def left(src, sem):
+        remote(src, src, sem, mr_sem.at[2], y_up).wait_send()
+
+    landed(max1, mr_sem.at[0])
+    left(max1, ms_sem.at[0])
+    top = max0[0]
+    for k in range(N_NEAR - 1):
+        top = jnp.maximum(top, max1[k])
+    max1v[0] = top
+    for k, part in enumerate(p_parts):
+        remote(max1v.at[0], max2.at[k], ms_sem.at[1], mr_sem.at[1], part).start()
 
     halo[2].wait()
     halo[3].wait()
@@ -207,62 +270,15 @@
         for t in range(2):
             rows = slice(8 * t, 8 * t + 8)
             for i in range(NF):
-                CH[i, z, rows, :] = (
+                ends = pltpu.roll(GY[i, rows, :], lax.rem(2 * NY - 4 - 8 * z, NY), 1)
+                a = jnp.where((lane < 2) | (lane == NY - 1), ends, CH[i, z, rows, :])
+                above = jnp.where(lane == NY - 1, pltpu.roll(ends, 1, 1), pltpu.roll(a, NY - 1, 1))
+                CH[i, z, rows, :] = (above - a) + (
                     FX[i * NZ + z, 8 * t + 1 : 8 * t + 9, :] - FX[i * NZ + z, rows, :]
                 )
         return 0
 
     lax.fori_loop(0, NZ, x_pass, 0)
-
-    def landed(dst, sem):
-        remote(dst, dst, ms_sem.at[2], sem, y_up).wait_recv()
-
-    def left(src, sem):
-        remote(src, src, sem, mr_sem.at[2], y_up).wait_send()
-
-    landed(max1, mr_sem.at[0])
-    left(max1, ms_sem.at[0])
-    top = max0[0]
-    for k in range(N_NEAR - 1):
-        top = jnp.maximum(top, max1[k])
-    max1v[0] = top
-    for k, part in enumerate(p_parts):
-        remote(max1v.at[0], max2.at[k], ms_sem.at[1], mr_sem.at[1], part).start()
-
-    halo[0].wait()
-    halo[1].wait()
-    for t in range(2):
-        rows = slice(8 * t, 8 * t + 8)
-        q = [[], [], [], []]
-        for i in range(NF):
-            mine = PK[i, rows, :]
-            other = recv_y[1, i, :, :].astype(F32)[rows]
-            q[0].append(mine)
-            q[1].append(pltpu.roll(mine, NY - 1, 1))
-            q[2].append(pltpu.roll(other, NY - 2, 1))
-            q[3].append(pltpu.roll(other, NY - 3, 1))
-        for i, a in enumerate(face(*q, 3)):
-            GY[i, rows, :] = a
-
-    def y_pass(z, _):
-        for t in range(2):
-            rows = slice(8 * t, 8 * t + 8)
-            q = [[], [], [], []]
-            for i in range(NF):
-                own = W[i * WZ + 2 + z, 8 + 8 * t : 16 + 8 * t, :]
-                low = pltpu.roll(recv_y[0, i, :, :].astype(F32)[rows], lax.rem(NY - 4 * z, NY), 1)
-                high = pltpu.roll(recv_y[1, i, :, :].astype(F32)[rows], 125 - 4 * z, 1)
-                q[0].append(jnp.where(lane < 2, low, pltpu.roll(own, 2, 1)))
-                q[1].append(jnp.where(lane < 1, pltpu.roll(low, NY - 1, 1), pltpu.roll(own, 1, 1)))
-                q[2].append(own)
-                q[3].append(jnp.where(lane == NY - 1, high, pltpu.roll(own, NY - 1, 1)))
-            for i, a in enumerate(face(*q, 3)):
-                end = pltpu.roll(GY[i, rows, :], 127 - 4 * z, 1)
-                above = jnp.where(lane == NY - 1, end, pltpu.roll(a, NY - 1, 1))
-                CH[i, z, rows, :] = CH[i, z, rows, :] + (above - a)
-        return 0
-
-    lax.fori_loop(0, NZ, y_pass, 0)
 
     halo[4].wait()
     halo[5].wait()
@@ -425,7 +441,8 @@
             pltpu.VMEM((NF, NZ, NX, NY), F32),
             pltpu.VMEM((NF * NZ, 24, NY), F32),
             pltpu.VMEM((NZ + 1, NF, NX, NY), F32),
-                pltpu.VMEM((NZ, NX, NY), F32),
+                pltpu.VMEM((3, NF * NZ, NX, NY), F32),
+        pltpu.VMEM((NZ, NX, NY), F32),
             pltpu.VMEM((NF, NX, NY), F32),
             pltpu.VMEM((NF, NX, NY), F32),
             pltpu.VMEM((NY, NY), F32),

time: 25.1 us -> 23.6 us (0.940)
  Pallas kernels: 24.4 us -> 22.8 us
    pallas_call x1, Pallas kernels: 23.5 us -> 22 us  [body(): pl.pallas_call(kernel, out_shape=tuple((pltpu.VMEM(*s) for s in shapes)),...]
where the time goes in v3:
time: 23.6 us; the launch traced here: 23.5 us
  Pallas kernels  22.8 us (97%)
  between operations  0.64 us (3%)
    pallas_call x1, Pallas kernels, body(): pl.pallas_call(kernel, out_shape=tuple((pltpu.VMEM(*s) for s in shapes)),...  22 us
    pallas_call x1, Pallas kernels, body(): pl.pallas_call(put_out, out_shape=tuple((jax.ShapeDtypeStruct(*s) for s i...  0.88 us

profile of v3, /device:TPU:1, one launch (start us, length us, event | category | flops | bytes accessed | tf_op | source)
XLA Modules:
  0.0 23.5 jit_solution(1701203957485683579)
XLA Ops:
  0.6 22.0 %shard_map.57 = (f32[1,5,16,16,128]{4,3,2,1,0:T(8,128)S(1)}, f32[1,3,1,16]{3,2,1,0:T(1,128)S(1)}, bf16[1,12,4,32]{3,2,1,0:T(4,128)(2,1)S(1)}, bf16[1,1,3,8]{3,2,1,0:T(4,128)(2,1)S(1)}) custom-call(f32[1,5,16,16,128]{4,3,2,1,0:T(8,128)} %state_ref.1, s32[16]{0:T(128)} %dir_ref.1), custom_call_target="tpu_custom_call" | custom-call | tf_op jit(solution)/shard_map/pallas_call | solution.py:433
  22.6 0.9 %shard_map.58 = (f32[1,5,16,16,128]{4,3,2,1,0:T(8,128)}, f32[1,3,1,16]{3,2,1,0:T(1,128)}, bf16[1,12,4,32]{3,2,1,0:T(4,128)(2,1)}, bf16[1,1,3,8]{3,2,1,0:T(4,128)(2,1)}) custom-call(f32[1,5,16,16,128]{4,3,2,1,0:T(8,128)S(1)} %get-tuple-element.12.new_in, f32[1,3,1,16]{3,2,1,0:T(1,128)S(1)} %get-tuple-element.13.view_in, ...), custom_call_target="tpu_custom_call" | custom-call | tf_op jit(solution)/shard_map/pallas_call | solution.py:467

commit v4 on v3

--- a/solution.py
+++ b/solution.py
@@ -70,7 +70,7 @@
 
 def kernel(
     state_ref, dir_ref, NEW, view_ref, fine_ref, coarse_ref,
-    S, W, CH, FX, FZ, QY, SN, PK, GY, VT, LH, SO,
+    S, W, CH, FX, FZ, QY, ST, CT, DT, RV, PK, GY, LH, SO,
     send_z, send_x, send_y, recv_z, recv_x, recv_y,
     max0, max1, max1v, max2, recv_v, recv_o,
     in_sem, out_sem, hs_sem, hr_sem, ms_sem, mr_sem, vs_sem, vr_sem, os_sem, or_sem,
@@ -130,7 +130,8 @@
     for n in range(CHUNKS):
         loads[n].wait()
         carry = lax.fori_loop(n * depth, (n + 1) * depth, prims, carry)
-    max0[0] = jnp.max(carry[0], axis=0, keepdims=True)
+    top = jnp.max(jnp.max(carry[0], axis=0, keepdims=True), axis=1, keepdims=True)
+    max0[0] = jnp.broadcast_to(top, (1, NY))
     pl.semaphore_wait(barrier, len(greeted))
 
     def remote(src, dst, ssem, rsem, part):
@@ -296,11 +297,19 @@
 
     lax.fori_loop(0, NZ, gather_change, 0)
 
-    facing = jnp.zeros((NX, NY), jnp.int32)
+    for h in range(2):
+        planes = slice(8 * h, 8 * h + 8)
+        ST[h] = jnp.transpose(S[0, 0, planes].reshape(NY, NY))
+        CT[h] = jnp.transpose(CH[0, planes].reshape(NY, NY))
+    cell_x = lane & (NX - 1)
+    facing = jnp.zeros((8, NY), jnp.int32)
     for x in range(NX):
-        facing = jnp.where(row16 == x, dir_ref[x], facing)
-    fraction = (gy * NY + lane16).astype(F32) / F32(NY * N_GY - 1)
-    dim = jnp.where(facing == 0, jnp.exp(-fraction), jnp.exp(-(1.0 - fraction)))
+        facing = jnp.where(cell_x == x, dir_ref[x], facing)
+    for n in range(NY // 8):
+        y = lax.broadcasted_iota(jnp.int32, (8, NY), 0) + (gy * NY + 8 * n)
+        fraction = y.astype(F32) / F32(NY * N_GY - 1)
+        dim = jnp.where(facing == 0, jnp.exp(-fraction), jnp.exp(-(1.0 - fraction)))
+        DT[8 * n : 8 * n + 8, :] = dim
     picks_from = lax.broadcasted_iota(jnp.int32, (NY, NY), 0)
     picks_to = lax.broadcasted_iota(jnp.int32, (NY, NY), 1)
     picks = (picks_from == 4 * picks_to) | (
@@ -310,89 +319,71 @@
 
     landed(max2, mr_sem.at[1])
     left(max2, ms_sem.at[1])
-    for k in range(N_NEAR - 1):
-        top = jnp.maximum(top, max2[k])
-    speed = jnp.max(top, axis=1, keepdims=True)
-    half_step = jnp.broadcast_to(0.5 * (0.8 / speed), (8, NY))
-
-    def lit(z, t):
-        rows = slice(8 * t, 8 * t + 8)
-        rho = S[0, 0, z, rows, :] - half_step * CH[0, z, rows, :]
-        snap = rho.astype(BF16).astype(F32)
-        SN[z, rows, :] = snap
-        return snap * dim[rows]
-
-    def folded(z, bit, t):
-        span = 8 << bit
-        if bit == 3:
-            a, b = lit(z, t), lit(z + 8, t)
-        else:
-            a, b = folded(z, bit + 1, t), folded(z + (1 << bit), bit + 1, t)
-        a = jnp.maximum(a, pltpu.roll(a, NY - span, 1))
-        b = jnp.maximum(b, pltpu.roll(b, span, 1))
-        return jnp.where(lane & span == 0, a, b)
-
-    halves = []
-    for t in range(2):
-        a = folded(0, 0, t)
-        for span in (4, 2, 1):
-            a = jnp.maximum(a, pltpu.roll(a, NY - span, 1))
-        halves.append(a)
-    VT[...] = jnp.transpose(jnp.concatenate(halves + [jnp.zeros((NY - NX, NY), F32)], axis=0))
+    rows = [max1v[0]] + [max2[k] for k in range(N_NEAR - 1)]
+    while len(rows) > 1:
+        rows = [jnp.maximum(p, q) for p, q in zip(rows[::2], rows[1::2])]
+    half_step = jnp.broadcast_to(0.5 * (0.8 / rows[0]), (8, NY))
+
+    view_ref[...] = jnp.zeros(view_ref.shape, F32)
+    fine_ref[...] = jnp.zeros(fine_ref.shape, BF16)
+    coarse_ref[...] = jnp.zeros(coarse_ref.shape, BF16)
 
     @pl.when(g < SLABS)
     def _():
+        for h in range(2):
+            lit = []
+            for n in range(NY // 8):
+                rows = slice(8 * n, 8 * n + 8)
+                rho = ST[h, rows, :] - half_step * CT[h, rows, :]
+                lit.append(rho.astype(BF16).astype(F32) * DT[rows, :])
+            while len(lit) > 1:
+                lit = [jnp.maximum(p, q) for p, q in zip(lit[::2], lit[1::2])]
+            RV[h] = jnp.max(lit[0], axis=0, keepdims=True)
         for k in range(N_GY):
             to = lax.rem(gy + k, N_GY)
             part = {"grp": SLABS, "gx": lax.axis_index("gx"), "gy": to}
-            remote(
-                VT.at[pl.ds(8 * to, 1)], recv_v.at[g * N_GY + gy], vs_sem, vr_sem, part
-            ).start()
-
-    tiles = []
-    whole = None
-    for zg in range(4):
-        for t in range(2):
-            rows = slice(8 * t, 8 * t + 8)
-            m = SN[4 * zg, rows, :]
-            for j in range(1, 4):
-                m = jnp.maximum(m, SN[4 * zg + j, rows, :])
-            for span in (1, 2):
-                m = jnp.maximum(m, pltpu.roll(m, NY - span, 1))
-            for span in (1, 2):
-                m = jnp.maximum(m, pltpu.roll(m, 8 - span, 0))
-            tiles.append(m)
-            whole = m if whole is None else jnp.maximum(whole, m)
-    for span in (4, 8):
-        whole = jnp.maximum(whole, pltpu.roll(whole, NY - span, 1))
-    whole = jnp.maximum(whole, pltpu.roll(whole, 4, 0))
-    left_hand = jnp.concatenate(tiles + [whole, whole], axis=0).astype(BF16)
-    LH[...] = jnp.dot(left_hand, picks, preferred_element_type=F32)
-    rows = jnp.concatenate([LH[pl.ds(0, 8, stride=4), :], LH[pl.ds(32, 8, stride=4), :]], axis=0)
-    last = jnp.broadcast_to(LH[64:65, :], (NX, NY))
-    SO[...] = jnp.where(lane16 < 32, rows, last).astype(BF16)
-
-    @pl.when(g < SLABS)
-    def _():
-        part = {"grp": SLABS, "gx": lax.axis_index("gx"), "gy": gy}
-        remote(SO, recv_o.at[g], os_sem, or_sem, part).start()
-
-    def update(z, _):
-        for i in range(NF):
+            remote(RV.at[to // 8], recv_v.at[g * N_GY + gy], vs_sem, vr_sem, part).start()
+
+        def update(i, z):
             for t in range(2):
                 rows = slice(8 * t, 8 * t + 8)
                 NEW[0, i, z, rows, :] = S[0, i, z, rows, :] - half_step * CH[i, z, rows, :]
-        return 0
-
-    view_ref[...] = jnp.zeros(view_ref.shape, F32)
-    fine_ref[...] = jnp.zeros(fine_ref.shape, BF16)
-    coarse_ref[...] = jnp.zeros(coarse_ref.shape, BF16)
-
-    @pl.when(g < SLABS)
-    def _():
-        lax.fori_loop(0, NZ, update, 0)
-        rows16 = recv_v.at[pl.ds(0, N_GY)]
-        left(rows16, vs_sem)
+
+        for z in range(NZ):
+            update(0, z)
+        tiles = []
+        whole = None
+        for zg in range(4):
+            for t in range(2):
+                rows = slice(8 * t, 8 * t + 8)
+                m = NEW[0, 0, 4 * zg, rows, :]
+                for j in range(1, 4):
+                    m = jnp.maximum(m, NEW[0, 0, 4 * zg + j, rows, :])
+                for span in (1, 2):
+                    m = jnp.maximum(m, pltpu.roll(m, NY - span, 1))
+                for span in (1, 2):
+                    m = jnp.maximum(m, pltpu.roll(m, 8 - span, 0))
+                tiles.append(m)
+                whole = m if whole is None else jnp.maximum(whole, m)
+        for span in (4, 8):
+            whole = jnp.maximum(whole, pltpu.roll(whole, NY - span, 1))
+        whole = jnp.maximum(whole, pltpu.roll(whole, 4, 0))
+        left_hand = jnp.concatenate(tiles + [whole, whole], axis=0).astype(BF16)
+        LH[...] = jnp.dot(left_hand, picks, preferred_element_type=F32)
+        rows = jnp.concatenate([LH[pl.ds(0, 8, stride=4), :], LH[pl.ds(32, 8, stride=4), :]], axis=0)
+        last = jnp.broadcast_to(LH[64:65, :], (NX, NY))
+        SO[...] = jnp.where(lane16 < 32, rows, last).astype(BF16)
+
+        part = {"grp": SLABS, "gx": lax.axis_index("gx"), "gy": gy}
+        remote(SO, recv_o.at[g], os_sem, or_sem, part).start()
+
+        def update_rest(z, _):
+            for i in range(1, NF):
+                update(i, z)
+            return 0
+
+        lax.fori_loop(0, NZ, update_rest, 0)
+        left(recv_v.at[pl.ds(0, N_GY)], vs_sem)
         left(SO, os_sem)
 
     @pl.when(is_viz)
@@ -408,7 +399,8 @@
             a = recv_v[s * N_GY]
             for k in range(1, N_GY):
                 a = jnp.maximum(a, recv_v[s * N_GY + k])
-            view_ref[0, s] = a[:, :NX]
+            a = pltpu.roll(jnp.broadcast_to(a, (8, NY)), lax.rem(NY - NX * lax.rem(gy, 8), NY), 1)
+            view_ref[0, s] = a[0:1, :NX]
         pltpu.make_async_copy(state_ref, NEW, out_sem).wait()
 
 
@@ -442,10 +434,12 @@
             pltpu.VMEM((NF * NZ, 24, NY), F32),
             pltpu.VMEM((NZ + 1, NF, NX, NY), F32),
                 pltpu.VMEM((3, NF * NZ, NX, NY), F32),
-        pltpu.VMEM((NZ, NX, NY), F32),
+            pltpu.VMEM((2, NY, NY), F32),
+            pltpu.VMEM((2, NY, NY), F32),
+            pltpu.VMEM((NY, NY), F32),
+            pltpu.VMEM((2, 1, NY), F32),
             pltpu.VMEM((NF, NX, NY), F32),
             pltpu.VMEM((NF, NX, NY), F32),
-            pltpu.VMEM((NY, NY), F32),
             pltpu.VMEM((80, NY), F32),
             pltpu.VMEM((NX, NY), BF16),
             pltpu.VMEM((2, NF, 2, NX, NY), BF16),

time: 23.6 us -> 23.1 us (0.979)
  Pallas kernels: 22.8 us -> 22.3 us
    pallas_call x1, Pallas kernels: 22 us -> 21.4 us  [body(): pl.pallas_call(kernel, out_shape=tuple((pltpu.VMEM(*s) for s in shapes)),...]
where the time goes in v4:
time: 23.1 us; the launch traced here: 23 us
  Pallas kernels  22.3 us (97%)
  between operations  0.64 us (3%)
    pallas_call x1, Pallas kernels, body(): pl.pallas_call(kernel, out_shape=tuple((pltpu.VMEM(*s) for s in shapes)),...  21.4 us
    pallas_call x1, Pallas kernels, body(): pl.pallas_call(put_out, out_shape=tuple((jax.ShapeDtypeStruct(*s) for s i...  0.88 us

profile of v4, /device:TPU:1, one launch (start us, length us, event | category | flops | bytes accessed | tf_op | source)
XLA Modules:
  0.0 23.0 jit_solution(15404627018058322364)
XLA Ops:
  0.6 21.4 %shard_map.57 = (f32[1,5,16,16,128]{4,3,2,1,0:T(8,128)S(1)}, f32[1,3,1,16]{3,2,1,0:T(1,128)S(1)}, bf16[1,12,4,32]{3,2,1,0:T(4,128)(2,1)S(1)}, bf16[1,1,3,8]{3,2,1,0:T(4,128)(2,1)S(1)}) custom-call(f32[1,5,16,16,128]{4,3,2,1,0:T(8,128)} %state_ref.1, s32[16]{0:T(128)} %dir_ref.1), custom_call_target="tpu_custom_call" | custom-call | tf_op jit(solution)/shard_map/pallas_call | solution.py:425
  22.1 0.9 %shard_map.58 = (f32[1,5,16,16,128]{4,3,2,1,0:T(8,128)}, f32[1,3,1,16]{3,2,1,0:T(1,128)}, bf16[1,12,4,32]{3,2,1,0:T(4,128)(2,1)}, bf16[1,1,3,8]{3,2,1,0:T(4,128)(2,1)}) custom-call(f32[1,5,16,16,128]{4,3,2,1,0:T(8,128)S(1)} %get-tuple-element.12.new_in, f32[1,3,1,16]{3,2,1,0:T(1,128)S(1)} %get-tuple-element.13.view_in, ...), custom_call_target="tpu_custom_call" | custom-call | tf_op jit(solution)/shard_map/pallas_call | solution.py:461

commit v5 on v4

--- a/solution.py
+++ b/solution.py
@@ -121,8 +121,6 @@
                 packed[2 * i + t] = jnp.where(
                     here, pltpu.roll(q, lax.rem(8 * z + 4, NY), 1), packed[2 * i + t]
                 )
-                for j, turn in enumerate((2, 1, NY - 1)):
-                    QY[j, i * NZ + z, rows, :] = pltpu.roll(q, turn, 1)
         return (top, *packed)
 
     zero = jnp.zeros((8, NY), F32)
@@ -175,6 +173,17 @@
         )
     for copy in halo:
         copy.start()
+
+    def y_shifts(z, _):
+        for i in range(NF):
+            for t in range(2):
+                rows = slice(8 * t, 8 * t + 8)
+                q = W[i * WZ + 2 + z, 8 + 8 * t : 16 + 8 * t, :]
+                for j, turn in enumerate((2, 1, NY - 1)):
+                    QY[j, i * NZ + z, rows, :] = pltpu.roll(q, turn, 1)
+        return 0
+
+    lax.fori_loop(0, NZ, y_shifts, 0)
 
     def z_face(p, _):
         for t in range(2):
@@ -339,10 +348,13 @@
             while len(lit) > 1:
                 lit = [jnp.maximum(p, q) for p, q in zip(lit[::2], lit[1::2])]
             RV[h] = jnp.max(lit[0], axis=0, keepdims=True)
-        for k in range(N_GY):
-            to = lax.rem(gy + k, N_GY)
-            part = {"grp": SLABS, "gx": lax.axis_index("gx"), "gy": to}
-            remote(RV.at[to // 8], recv_v.at[g * N_GY + gy], vs_sem, vr_sem, part).start()
+        half, pair = gy // 8, lax.rem(gy, 8) // 2
+        for z_half in (1 - half, half):
+            for k in (2, 1, 3, 0):
+                for core in range(2):
+                    to = 8 * z_half + 2 * lax.rem(pair + k, 4) + core
+                    part = {"grp": SLABS, "gx": lax.axis_index("gx"), "gy": to}
+                    remote(RV.at[z_half], recv_v.at[g * N_GY + gy], vs_sem, vr_sem, part).start()
 
         def update(i, z):
             for t in range(2):
@@ -396,9 +408,10 @@
             coarse_ref[0, 0, s : s + 1, :] = block[0:1, 32:40]
         landed(recv_v, vr_sem)
         for s in range(SLABS):
-            a = recv_v[s * N_GY]
-            for k in range(1, N_GY):
-                a = jnp.maximum(a, recv_v[s * N_GY + k])
+            rows = [recv_v[s * N_GY + k] for k in range(N_GY)]
+            while len(rows) > 1:
+                rows = [jnp.maximum(p, q) for p, q in zip(rows[::2], rows[1::2])]
+            a = rows[0]
             a = pltpu.roll(jnp.broadcast_to(a, (8, NY)), lax.rem(NY - NX * lax.rem(gy, 8), NY), 1)
             view_ref[0, s] = a[0:1, :NX]
         pltpu.make_async_copy(state_ref, NEW, out_sem).wait()

time: 23.1 us -> 23 us (level)
  no operation moved by 1% of the time
where the time goes in v5:
time: 23 us; the launch traced here: 22.9 us
  Pallas kernels  22.3 us (97%)
  between operations  0.64 us (3%)
    pallas_call x1, Pallas kernels, body(): pl.pallas_call(kernel, out_shape=tuple((pltpu.VMEM(*s) for s in shapes)),...  21.4 us
    pallas_call x1, Pallas kernels, body(): pl.pallas_call(put_out, out_shape=tuple((jax.ShapeDtypeStruct(*s) for s i...  0.88 us

profile of v5, /device:TPU:1, one launch (start us, length us, event | category | flops | bytes accessed | tf_op | source)
XLA Modules:
  0.0 22.9 jit_solution(1295590738275659714)
XLA Ops:
  0.6 21.4 %shard_map.57 = (f32[1,5,16,16,128]{4,3,2,1,0:T(8,128)S(1)}, f32[1,3,1,16]{3,2,1,0:T(1,128)S(1)}, bf16[1,12,4,32]{3,2,1,0:T(4,128)(2,1)S(1)}, bf16[1,1,3,8]{3,2,1,0:T(4,128)(2,1)S(1)}) custom-call(f32[1,5,16,16,128]{4,3,2,1,0:T(8,128)} %state_ref.1, s32[16]{0:T(128)} %dir_ref.1), custom_call_target="tpu_custom_call" | custom-call | tf_op jit(solution)/shard_map/pallas_call | solution.py:438
  22.0 0.9 %shard_map.58 = (f32[1,5,16,16,128]{4,3,2,1,0:T(8,128)}, f32[1,3,1,16]{3,2,1,0:T(1,128)}, bf16[1,12,4,32]{3,2,1,0:T(4,128)(2,1)}, bf16[1,1,3,8]{3,2,1,0:T(4,128)(2,1)}) custom-call(f32[1,5,16,16,128]{4,3,2,1,0:T(8,128)S(1)} %get-tuple-element.12.new_in, f32[1,3,1,16]{3,2,1,0:T(1,128)S(1)} %get-tuple-element.13.view_in, ...), custom_call_target="tpu_custom_call" | custom-call | tf_op jit(solution)/shard_map/pallas_call | solution.py:474
